TPU v7x, 32 devices: a whole 2x2x4 slice. The times are simulated.
32 devices in a mesh: row: 8 (over y, x, core), col: 4 (over z).
Axes of the slice: x: 2, y: 2, z: 4, core: 2. Of those that a mesh axis runs over, the one named last changes fastest.
Arguments:
- question_vectors: bfloat16 [512, 2048], P('row', 'col'), may hold values from -0.5 to 0.5
- document_vectors: bfloat16 [512, 2048], P('col', 'row'), may hold values from -0.5 to 0.5
- positive: int32 [512], P('row'), may hold values from 0 to 511
- tokens: bfloat16 [4096, 2048], P(('row', 'col')), may hold values from -6 to 6
- expert_ids: int32 [4096, 8], P(('row', 'col')), may hold values from 0 to 31, all different within a row; in each aligned block of 128 rows (0 to 127, 128 to 255, ...) at most 36 rows name the same one
- route_weights: float32 [4096, 8], P(('row', 'col')), may hold values from 0.03 to 0.3
- expert_gate_up: bfloat16 [32, 2048, 1536], P(('row', 'col')), may hold values from -0.125 to 0.125
- expert_down: bfloat16 [32, 768, 2048], P(('row', 'col')), may hold values from -0.21875 to 0.21875
Outputs:
- passage_grad: float32 [512, 2048], P('col', 'row')
- token_grad: bfloat16 [4096, 2048], P(('row', 'col'))
- gate_up_grad: bfloat16 [32, 2048, 1536], P(('row', 'col'))
- down_grad: bfloat16 [32, 768, 2048], P(('row', 'col'))
Inputs may be any that keep to these rules, and one draw needn't show every extreme that they name: `expert_ids`: each token names 8 different experts; among the 128 tokens of one device no expert is named more than 36 times, a bound that some block reaches.
All inputs are finite; a program needn't handle non-finite values.
Results may differ from a plain program's by a relative error of at most 0.018.
Values may be sent and summed in bfloat16 or wider, within the bound.
A program may use at most 192 MiB of HBM per device.

v0:
```python
import functools

import jax
import jax.numpy as jnp
from jax import lax
from jax.experimental import pallas as pl
from jax.experimental.pallas import tpu as pltpu
from jax.sharding import PartitionSpec as P

SEQ_LEN = 8
LANES = 128
CHUNKS = 4
VMEM_LIMIT = 67_000_000

sharpness_divisor = 0.02

BF = jnp.bfloat16
F32 = jnp.float32
MESH = pl.DeviceIdType.MESH


def contract(a, b, da, db):
    return lax.dot_general(a, b, (((da,), (db,)), ((), ())), preferred_element_type=F32)


def span(index, size):
    return pl.ds(pl.multiple_of(index * size, size), size)


def remote(src, dst, send_sem, recv_sem, to):
    return pltpu.make_async_remote_copy(
        src_ref=src, dst_ref=dst, send_sem=send_sem, recv_sem=recv_sem,
        device_id=to, device_id_type=MESH,
    )


def greet(rows, cols):
    row, col = lax.axis_index("row"), lax.axis_index("col")
    barrier = pltpu.get_barrier_semaphore()
    for s in range(1, rows):
        pl.semaphore_signal(
            barrier, inc=1, device_id=(lax.rem(row + s, rows), col), device_id_type=MESH
        )
    for s in range(1, cols):
        pl.semaphore_signal(
            barrier, inc=1, device_id=(row, lax.rem(col + s, cols)), device_id_type=MESH
        )
    pl.semaphore_wait(barrier, rows + cols - 2)


def dispatch_kernel(
    rows, cols, cap,
    tok_ref, doc_ref, qry_ref, meta_ref, wgu_ref,
    x_ref, docs_ref, qrys_ref, metas_ref, proj_ref, dm_ref,
    tokc, packed, w, own_sem, w_sem, zs, zr, gs, gr, rs, ds, dr,
):
    row, col = lax.axis_index("row"), lax.axis_index("col")
    n_tok, width = tok_ref.shape
    n_doc, w_doc = doc_ref.shape
    n_qry, w_qry = qry_ref.shape
    top = 8
    step = width // CHUNKS
    block = cols * cap
    chips = rows // 2
    core = lax.rem(row, 2)
    chip = lax.div(row, 2)
    sibling = row + 1 - 2 * core

    def doc_strip(r):
        return docs_ref.at[:, span(r, w_doc)]

    def qry_strip(r):
        return qrys_ref.at[span(r, n_qry), :]

    def meta_strip(r):
        return metas_ref.at[pl.ds(r * cols, cols)]

    strips = (meta_strip, doc_strip, qry_strip)

    def line_piece(kind, c):
        if kind == 0:
            return meta_ref, metas_ref.at[row * cols + c]
        if kind == 1:
            return doc_ref, docs_ref.at[span(c, n_doc), span(row, w_doc)]
        if kind == 2:
            return qry_ref, qrys_ref.at[span(row, n_qry), span(c, w_qry)]
        f = kind - 3
        part = pl.ds(f * step, step)
        return tok_ref.at[:, part], tokc.at[span(c, n_tok), part]

    def along_line(kind, s, origin, to):
        src, dst = line_piece(kind, origin)
        return remote(src, dst, zs.at[kind, s], zr.at[kind, origin], (row, to))

    own = []
    for kind in range(3 + CHUNKS):
        src, dst = line_piece(kind, col)
        own.append(pltpu.make_async_copy(src, dst, own_sem.at[kind]))
    loads = [
        pltpu.make_async_copy(wgu_ref.at[span(f, step)], w.at[span(f, step)], w_sem.at[f])
        for f in range(CHUNKS)
    ]
    for copy in own:
        copy.start()
    for copy in loads:
        copy.start()
    greet(rows, cols)
    for kind in range(3 + CHUNKS):
        for s in range(1, cols):
            along_line(kind, s, col, lax.rem(col + s, cols)).start()

    def line_arrived(kind):
        own[kind].wait()
        for s in range(1, cols):
            origin = lax.rem(col + s, cols)
            along_line(kind, s, origin, origin).wait_recv()

    def peer(s):
        return 2 * lax.rem(chip + s, chips) + core

    def direct(kind, s, origin, to):
        return remote(strips[kind](origin), strips[kind](origin), gs.at[kind, s],
                      gr.at[kind, origin], (to, col))

    def relay(kind, s, origin):
        return remote(strips[kind](origin), strips[kind](origin), rs.at[kind, s],
                      gr.at[kind, origin], (sibling, col))

    for kind in range(3):
        line_arrived(kind)
        for s in range(1, chips):
            direct(kind, s, row, peer(s)).start()
        direct(kind, 0, row, sibling).start()

    target = (
        lax.broadcasted_iota(jnp.int32, (rows, n_tok), 0) * cols + col
    ).astype(F32)
    before = (
        lax.broadcasted_iota(jnp.int32, (n_tok, n_tok), 0)
        < lax.broadcasted_iota(jnp.int32, (n_tok, n_tok), 1)
    ).astype(BF)
    slot = lax.broadcasted_iota(jnp.int32, (block, n_tok), 0).astype(F32)
    for c in range(cols):
        ids = metas_ref[row * cols + c]
        hit = jnp.zeros((rows, n_tok), F32)
        for k in range(top):
            hit = hit + (ids[k : k + 1, :] == target).astype(F32)
        rank = contract(hit.astype(BF), before, 1, 0)
        place = jnp.where(hit > 0.5, rank + float(c * cap), -1.0)
        for r in range(rows):
            dm_ref[r * block : (r + 1) * block, c * n_tok : (c + 1) * n_tok] = jnp.where(
                slot == place[r : r + 1, :], 1.0, 0.0
            ).astype(BF)

    def outgoing(f, s, origin, to):
        part = pl.ds(f * step, step)
        return remote(packed.at[span(to, block), part], x_ref.at[span(origin, block), part],
                      ds.at[f, s], dr.at[f, origin], (to, col))

    def kept(f):
        part = pl.ds(f * step, step)
        return pltpu.make_async_copy(
            packed.at[span(row, block), part], x_ref.at[span(row, block), part],
            own_sem.at[3 + CHUNKS + f],
        )

    pair = 2 * block
    for f in range(CHUNKS):
        line_arrived(3 + f)
        part = slice(f * step, (f + 1) * step)

        @pl.loop(0, rows // 2)
        def _(m):
            packed[span(m, pair), part] = contract(
                dm_ref[span(m, pair), :], tokc[:, part], 1, 0
            ).astype(BF)

        for s in range(1, rows):
            outgoing(f, s, row, lax.rem(row + s, rows)).start()
        kept(f).start()

    for kind in range(3):
        for s in range(1, chips):
            origin = peer(s)
            direct(kind, s, origin, origin).wait_recv()
            relay(kind, s, origin).start()

    hidden2 = proj_ref.shape[1]
    tile = 512
    for f in range(CHUNKS):
        loads[f].wait()
        kept(f).wait()
        for s in range(1, rows):
            origin = lax.rem(row + s, rows)
            outgoing(f, s, origin, origin).wait_recv()
        part = slice(f * step, (f + 1) * step)

        @pl.loop(0, hidden2 // tile)
        def _(n):
            term = contract(x_ref[:, part], w[part, span(n, tile)], 1, 0)
            if f == 0:
                proj_ref[:, span(n, tile)] = term
            else:
                proj_ref[:, span(n, tile)] += term

    for kind in range(3):
        direct(kind, 0, sibling, sibling).wait_recv()
        for s in range(1, chips):
            origin = 2 * lax.rem(chip + s, chips) + 1 - core
            relay(kind, s, origin).wait_recv()
    for kind in range(3):
        for s in range(1, chips):
            direct(kind, s, row, peer(s)).wait_send()
            relay(kind, s, peer(s)).wait_send()
        direct(kind, 0, row, sibling).wait_send()
    for kind in range(3 + CHUNKS):
        for s in range(1, cols):
            along_line(kind, s, col, lax.rem(col + s, cols)).wait_send()
    for f in range(CHUNKS):
        for s in range(1, rows):
            outgoing(f, s, row, lax.rem(row + s, rows)).wait_send()


def dispatch(rows, cols, cap, tokens, documents, questions, meta, gate_up):
    n_tok, width = tokens.shape
    n_doc, w_doc = documents.shape
    n_qry, w_qry = questions.shape
    slots = rows * cols * cap
    hidden2 = gate_up.shape[1]
    dma = pltpu.SemaphoreType.DMA
    vmem = pl.BlockSpec(memory_space=pltpu.VMEM)
    hbm = pl.BlockSpec(memory_space=pl.ANY)
    return pl.pallas_call(
        functools.partial(dispatch_kernel, rows, cols, cap),
        out_shape=(
            jax.ShapeDtypeStruct((slots, width), BF),
            jax.ShapeDtypeStruct((cols * n_doc, rows * w_doc), BF),
            jax.ShapeDtypeStruct((rows * n_qry, cols * w_qry), BF),
            jax.ShapeDtypeStruct((rows * cols,) + meta.shape, F32),
            jax.ShapeDtypeStruct((slots, hidden2), F32),
            jax.ShapeDtypeStruct((slots, cols * n_tok), BF),
        ),
        in_specs=[vmem] * 4 + [hbm],
        out_specs=[vmem, hbm, hbm, vmem, vmem, vmem],
        scratch_shapes=[
            pltpu.VMEM((cols * n_tok, width), BF),
            pltpu.VMEM((slots, width), BF),
            pltpu.VMEM((width, hidden2), BF),
            dma((3 + 2 * CHUNKS,)),
            dma((CHUNKS,)),
            dma((3 + CHUNKS, cols)),
            dma((3 + CHUNKS, cols)),
            dma((3, rows)),
            dma((3, rows)),
            dma((3, rows)),
            dma((CHUNKS, rows)),
            dma((CHUNKS, rows)),
        ],
        compiler_params=pltpu.CompilerParams(
            collective_id=0, has_side_effects=True, vmem_limit_bytes=VMEM_LIMIT
        ),
        name="dispatch",
    )(tokens, documents, questions, meta, gate_up)


def combine_kernel(
    rows, cols,
    pre_ref, dmt_ref, cot_ref, wgu_ref, xin_ref,
    tok_ref, gug_ref,
    w, x, back, ret, comb, parts, stage,
    load_sem, own_sem, es, er, fs, fr, out_sem,
):
    row, col = lax.axis_index("row"), lax.axis_index("col")
    slots = pre_ref.shape[0]
    block = slots // rows
    width = wgu_ref.shape[0]
    n_tok = cot_ref.shape[0]
    step = width // CHUNKS

    loads = [
        pltpu.make_async_copy(wgu_ref.at[span(f, step)], w.at[span(f, step)], load_sem.at[f])
        for f in range(CHUNKS)
    ]
    loads.append(pltpu.make_async_copy(xin_ref, x, load_sem.at[CHUNKS]))
    for copy in loads:
        copy.start()
    greet(rows, cols)

    def returning(f, s, origin, to):
        part = pl.ds(f * step, step)
        return remote(back.at[span(to, block), part], ret.at[span(origin, block), part],
                      es.at[f, s], er.at[f, origin], (to, col))

    def kept(f):
        part = pl.ds(f * step, step)
        return pltpu.make_async_copy(
            back.at[span(row, block), part], ret.at[span(row, block), part], own_sem.at[f]
        )

    def home(f, s, origin, to):
        part = pl.ds(f * step, step)
        return remote(comb.at[span(to, n_tok), part], parts.at[origin, :, part],
                      fs.at[f, s], fr.at[f, origin], (row, to))

    tile = 256
    for f in range(CHUNKS):
        loads[f].wait()

        @pl.loop(0, step // tile)
        def _(n):
            back[:, pl.ds(pl.multiple_of(f * step + n * tile, tile), tile)] = contract(
                pre_ref[...], w[pl.ds(pl.multiple_of(f * step + n * tile, tile), tile), :], 1, 1
            ).astype(BF)

        for s in range(1, rows):
            returning(f, s, row, lax.rem(row + s, rows)).start()
        kept(f).start()
    loads[CHUNKS].wait()

    def grad_tile(i):
        here = slice(i * step, (i + 1) * step)
        stage[i % 2] = contract(x[:, here], pre_ref[...], 0, 0).astype(BF)

    def grad_out(i):
        return pltpu.make_async_copy(
            stage.at[i % 2], gug_ref.at[pl.ds(i * step, step)], out_sem.at[i % 2]
        )

    def merge(f):
        kept(f).wait()
        for s in range(1, rows):
            origin = lax.rem(row + s, rows)
            returning(f, s, origin, origin).wait_recv()
        part = slice(f * step, (f + 1) * step)
        comb[:, part] = contract(dmt_ref[...], ret[:, part], 1, 0).astype(BF)
        for s in range(1, cols):
            home(f, s, col, lax.rem(col + s, cols)).start()

    def finish(f):
        part = slice(f * step, (f + 1) * step)
        total = cot_ref[:, part].astype(F32) + comb[span(col, n_tok), part].astype(F32)
        for s in range(1, cols):
            origin = lax.rem(col + s, cols)
            home(f, s, origin, origin).wait_recv()
            total = total + parts[origin, :, part].astype(F32)
        tok_ref[:, part] = total.astype(BF)

    for i in range(CHUNKS):
        if i >= 2:
            grad_out(i - 2).wait()
        grad_tile(i)
        grad_out(i).start()
        merge(i)
        if i >= 1:
            finish(i - 1)
    finish(CHUNKS - 1)
    for i in range(CHUNKS - 2, CHUNKS):
        grad_out(i).wait()
    for f in range(CHUNKS):
        for s in range(1, rows):
            returning(f, s, row, lax.rem(row + s, rows)).wait_send()
        for s in range(1, cols):
            home(f, s, col, lax.rem(col + s, cols)).wait_send()


def combine(rows, cols, pre_grad, dispatch_t, cot_tok, gate_up, slot_inputs):
    slots, hidden2 = pre_grad.shape
    n_tok, width = cot_tok.shape
    step = width // CHUNKS
    dma = pltpu.SemaphoreType.DMA
    vmem = pl.BlockSpec(memory_space=pltpu.VMEM)
    hbm = pl.BlockSpec(memory_space=pl.ANY)
    return pl.pallas_call(
        functools.partial(combine_kernel, rows, cols),
        out_shape=(
            jax.ShapeDtypeStruct((n_tok, width), BF),
            jax.ShapeDtypeStruct((width, hidden2), BF),
        ),
        in_specs=[vmem, vmem, vmem, hbm, hbm],
        out_specs=[vmem, hbm],
        scratch_shapes=[
            pltpu.VMEM((width, hidden2), BF),
            pltpu.VMEM((slots, width), BF),
            pltpu.VMEM((slots, width), BF),
            pltpu.VMEM((slots, width), BF),
            pltpu.VMEM((cols * n_tok, width), BF),
            pltpu.VMEM((cols, n_tok, width), BF),
            pltpu.VMEM((2, step, hidden2), BF),
            dma((CHUNKS + 1,)),
            dma((CHUNKS,)),
            dma((CHUNKS, rows)),
            dma((CHUNKS, rows)),
            dma((CHUNKS, cols)),
            dma((CHUNKS, cols)),
            dma((2,)),
        ],
        compiler_params=pltpu.CompilerParams(
            collective_id=1, has_side_effects=True, vmem_limit_bytes=VMEM_LIMIT
        ),
        name="combine",
    )(pre_grad, dispatch_t, cot_tok, gate_up, slot_inputs)


def shards(
    question_vectors,
    document_vectors,
    positive,
    tokens,
    expert_ids,
    route_weights,
    expert_gate_up,
    expert_down,
):
    rows = lax.axis_size("row")
    cols = lax.axis_size("col")
    row = lax.axis_index("row")
    col = lax.axis_index("col")
    devices_all = rows * cols
    me = row * cols + col
    n_tok, width = tokens.shape
    top = expert_ids.shape[1]
    experts_all = devices_all * expert_gate_up.shape[0]
    cap = max(2, (n_tok * top * 9 + 8 * experts_all - 1) // (8 * experts_all))
    block = cols * cap
    hidden_width = expert_down.shape[1]
    gate_up = expert_gate_up[0]
    down = expert_down[0]

    n_qry = positive.shape[0]
    pos_rows = -(-n_qry // (8 * LANES)) * 8
    pos = jnp.pad(positive, (0, pos_rows * LANES - n_qry)).astype(F32).reshape(pos_rows, LANES)
    meta = jnp.concatenate([expert_ids.T.astype(F32), route_weights.T, pos], axis=0)
    slot_inputs, docs, qrys, metas, projected, dm = dispatch(
        rows, cols, cap, tokens, document_vectors, question_vectors, meta, gate_up
    )

    ids = metas[:, :top].astype(jnp.int32)
    weights = metas[:, top : 2 * top]
    positive_all = metas.reshape(rows, cols, -1, LANES)[:, 0, 2 * top :].reshape(rows, -1)
    positive_all = positive_all[:, :n_qry].reshape(-1).astype(jnp.int32)

    scores = contract(qrys, docs, 1, 1) / sharpness_divisor
    peak = jnp.max(scores, axis=1, keepdims=True)
    grown = jnp.exp(scores - peak)
    total = jnp.sum(grown, axis=1, keepdims=True)
    onehot = (
        positive_all[:, None] == jnp.arange(docs.shape[0], dtype=jnp.int32)[None, :]
    ).astype(F32)
    dscore = ((grown / total - onehot) / sharpness_divisor).astype(BF)
    cot = (contract(dscore, docs, 1, 0) / SEQ_LEN).astype(BF)
    n_doc, w_doc = document_vectors.shape
    passage_grad = contract(
        lax.dynamic_slice_in_dim(dscore, col * n_doc, n_doc, 1),
        lax.dynamic_slice_in_dim(qrys, row * w_doc, w_doc, 1),
        0, 0,
    )

    mine = ids == me
    chosen = jnp.any(mine, axis=1)
    weight = jnp.sum(jnp.where(mine, weights, 0.0), axis=1)
    earlier = (
        lax.broadcasted_iota(jnp.int32, (n_tok, n_tok), 0)
        < lax.broadcasted_iota(jnp.int32, (n_tok, n_tok), 1)
    ).astype(BF)
    rank = contract(chosen.astype(BF), earlier, 1, 0).astype(jnp.int32)
    first = jnp.tile(jnp.arange(cols, dtype=jnp.int32) * cap, rows)[:, None]
    place = jnp.where(chosen, first + rank, -1).reshape(rows, 1, cols * n_tok)
    line_weight = weight.reshape(rows, 1, cols * n_tok)
    placed = jnp.where(
        place == jnp.arange(block, dtype=jnp.int32)[None, :, None], line_weight, 0.0
    ).astype(BF)
    line_q = cols * n_tok // SEQ_LEN
    grouped = (
        lax.broadcasted_iota(jnp.int32, (cols * n_tok, line_q), 0) // SEQ_LEN
        == lax.broadcasted_iota(jnp.int32, (cols * n_tok, line_q), 1)
    ).astype(BF)
    spread = contract(placed.reshape(-1, cols * n_tok), grouped, 1, 0).astype(BF)
    spread = spread.reshape(rows, block, line_q)

    gate_part = projected[:, :hidden_width]
    up_part = projected[:, hidden_width:]
    sigmoid_gate = jax.nn.sigmoid(gate_part)
    activated = gate_part * sigmoid_gate
    hidden = (activated * up_part).astype(BF)
    cot_down = contract(cot, down, 1, 1).astype(BF).reshape(rows, line_q, hidden_width)
    hidden_grad = lax.dot_general(
        spread, cot_down, (((2,), (1,)), ((0,), (0,))), preferred_element_type=F32
    ).reshape(-1, hidden_width)
    slope = sigmoid_gate * (1.0 + gate_part * (1.0 - sigmoid_gate))
    pre_grad = jnp.concatenate(
        [hidden_grad * up_part * slope, hidden_grad * activated], axis=1
    ).astype(BF)

    per_dev = n_tok // SEQ_LEN
    cot_own = lax.dynamic_slice_in_dim(cot, me * per_dev, per_dev, 0)
    cot_tok = jnp.repeat(cot_own, SEQ_LEN, axis=0)
    token_grad, gate_up_grad = combine(
        rows, cols, pre_grad, dm.T, cot_tok, gate_up, slot_inputs
    )

    hidden_by_query = lax.dot_general(
        spread, hidden.reshape(rows, block, hidden_width), (((1,), (1,)), ((0,), (0,))),
        preferred_element_type=F32,
    ).astype(BF).reshape(-1, hidden_width)
    down_grad = contract(hidden_by_query, cot, 0, 0).astype(BF)
    return (passage_grad, token_grad, gate_up_grad[None], down_grad[None])


def solution(mesh):
    in_specs = (
        P("row", "col"),
        P("col", "row"),
        P("row"),
        P(("row", "col"), None),
        P(("row", "col"), None),
        P(("row", "col"), None),
        P(("row", "col"), None, None),
        P(("row", "col"), None, None),
    )
    out_specs = (
        P("col", "row"),
        P(("row", "col"), None),
        P(("row", "col"), None, None),
        P(("row", "col"), None, None),
    )
    return jax.shard_map(shards, mesh=mesh, in_specs=in_specs, out_specs=out_specs, check_vma=False)
```

profile of v0, /device:TPU:0, one launch (start us, length us, event | category | flops | bytes accessed | tf_op | source)
XLA Modules:
  0.0 212.0 jit_solution(5241071349212070637)
XLA Ops:
  0.6 0.7 convert_bitcast_fusion
  1.3 0.7 convert_bitcast_fusion.1
  2.0 1.3 pad_maximum_fusion.1.meta_ref
  3.3 99.7 %dispatch.1 = (bf16[1152,2048]{1,0:T(8,128)(2,1)}, bf16[512,2048]{1,0:T(8,128)(2,1)}, bf16[512,2048]{1,0:T(8,128)(2,1)}, f32[32,24,128]{2,1,0:T(8,128)}, f32[115...) custom-call(bf16[128,2048]{1,0:T(8,128)(2,1)} %tok_ref.1, bf16[128,256]{1,0:T(8,128)(2,1)} %doc_ref.1, bf16[64,512]{1,0:T(8,128)(2,1)} %qry_ref.1, ...), custom_call_target="tpu_custom_call" | custom-call | tf_op jit(solution)/shard_map/dispatch/pallas_call | solution.py:233
  103.0 3.6 %fusion.28 = (f32[512]{0:T(512)S(1)}, f32[512,512]{0,1:T(8,128)S(1)}) fusion(bf16[512,2048]{1,0:T(8,128)(2,1)} %get-tuple-element.12, bf16[512,2048]{1,0:T(8,128)(2,1)} %get-tuple-element.13), kind=kOutput, calls=%fused_computation.59 | convolution fusion | flops 1074265600 | bytes 5244928 | tf_op jit(solution)/shard_map/dot_general | solution.py:23
  106.6 0.1 convert_element_type.61
  106.7 0.2 fusion.13
  106.9 0.3 multiply_convert_fusion.2
  107.2 1.8 fusion.14
  109.0 3.0 %multiply_convert_fusion = bf16[512,2048]{1,0:T(8,128)(2,1)S(1)} fusion(bf16[512,512]{0,1:T(8,128)(2,1)S(1)} %multiply_convert_fusion.2, bf16[512,2048]{1,0:T(8,128)(2,1)} %get-tuple-element.13), kind=kOutput, calls=%fused_computation | convolution fusion | flops 1075838976 | bytes 4718592 | tf_op jit(solution)/shard_map/dot_general | solution.py:23
  112.1 0.0 copy-start.4
  112.1 1.9 fusion.8
  114.0 0.1 fusion.27
  114.0 0.1 select_reduce_fusion
  114.1 0.1 eq.53
  114.2 0.1 add.35
  114.3 0.1 fusion.12
  114.4 0.3 fusion.7
  114.8 0.7 convolution_convert_fusion.1
  115.4 0.4 reshape.56
  115.8 0.7 fusion.17
  116.5 5.0 %fusion.1 = (bf16[1152,768]{1,0:T(8,128)(2,1)S(1)}, bf16[1152,768]{1,0:T(8,128)(2,1)S(1)}, bf16[1152,768]{1,0:T(8,128)(2,1)}) fusion(f32[8,144,768]{2,1,0:T(8,128)S(1)} %fusion.17, f32[1152,1536]{1,0:T(8,128)} %get-tuple-element.15), kind=kLoop, calls=%fused_computation.5 | loop fusion | flops 13271040 | bytes 15925248 | tf_op jit(solution)/shard_map/convert
  121.5 2.1 pad_maximum_fusion.pre_ref
  123.6 1.4 copy.16
  125.0 0.8 constant_dynamic-slice_fusion
  125.8 0.9 broadcast_bitcast_fusion.cot_ref
  126.7 76.1 %combine.1 = (bf16[128,2048]{1,0:T(8,128)(2,1)}, bf16[2048,1536]{1,0:T(8,128)(2,1)}) custom-call(bf16[1152,1536]{1,0:T(8,128)(2,1)} %pad_maximum_fusion.pre_ref, bf16[512,1152]{1,0:T(8,128)(2,1)} %bitcast.63, bf16[128,2048]{1,0:T(8,128)(2,1)} %broadcast_bitcast_fusion.cot_ref, bf16[2048,1536]{1,0:T(8,128)(2,1)} %bitcast.58, ...), custom_call_target="tpu_custom_call" | custom-call | tf_op jit(solution)/shard_map/combine/pallas_call | solution.py:373
  202.8 2.1 convolution_convert_fusion.2
  204.9 0.1 copy-done.5
  205.0 3.5 %fusion.6 = bf16[1,768,2048]{2,1,0:T(8,128)(2,1)} fusion(bf16[512,768]{1,0:T(8,128)(2,1)S(1)} %bitcast.65, bf16[512,2048]{1,0:T(8,128)(2,1)S(1)} %copy-done.5), kind=kOutput, calls=%fused_computation.13 | convolution fusion | flops 1612185600 | bytes 6029312 | tf_op jit(solution)/shard_map/dot_general | solution.py:23
  208.5 0.8 copy.27
  209.3 2.7 %copy.28 = bf16[1,2048,1536]{2,1,0:T(8,128)(2,1)} copy(bf16[1,2048,1536]{2,1,0:T(8,128)(2,1)S(1)} %bitcast.62) | data formatting | bytes 12582912
  (27 shorter events, 0.1 us)
Async XLA Ops:
  103.0 3.6 %copy-start.3 = (f32[32,24,128]{2,1,0:T(8,128)S(1)}, f32[32,24,128]{2,1,0:T(8,128)}, u32[]{:S(2)}) copy-start(f32[32,24,128]{2,1,0:T(8,128)} %get-tuple-element.14) | copy-start | bytes 1179652
  109.0 3.0 %copy-start.6 = (bf16[1,768,2048]{2,1,0:T(8,128)(2,1)S(1)}, bf16[1,768,2048]{2,1,0:T(8,128)(2,1)}, u32[]{:S(2)}) copy-start(bf16[1,768,2048]{2,1,0:T(8,128)(2,1)} %param.15) | copy-start | bytes 9437188
  112.1 1.9 copy-start.4
  115.8 5.7 %copy-start = (bf16[8,144,64]{1,0,2:T(8,128)(2,1)}, bf16[8,144,64]{1,0,2:T(8,128)(2,1)S(1)}, u32[]{:S(2)}) copy-start(bf16[8,144,64]{1,0,2:T(8,128)(2,1)S(1)} %reshape.56) | copy-start | bytes 442372
  121.5 2.1 copy-start.1
  202.8 2.2 %copy-start.5 = (bf16[512,2048]{1,0:T(8,128)(2,1)S(1)}, bf16[512,2048]{1,0:T(8,128)(2,1)}, u32[]{:S(2)}) copy-start(bf16[512,2048]{1,0:T(8,128)(2,1)} %copy-done.4) | copy-start | bytes 6291460
  202.8 6.5 %slice-start = ((s8[6291456]{0:T(1024)(128)(4,1)}), s8[4194304]{0:T(1024)(128)(4,1)S(1)}, s32[]{:S(2)}) async-start(s8[6291456]{0:T(1024)(128)(4,1)} %bitcast.60), calls=%async_computation | async-start | bytes 8388608
  205.0 3.5 %copy-start.2 = (bf16[128,2048]{1,0:T(8,128)(2,1)S(1)}, bf16[128,2048]{1,0:T(8,128)(2,1)}, u32[]{:S(2)}) copy-start(bf16[128,2048]{1,0:T(8,128)(2,1)} %get-tuple-element.34) | copy-start | bytes 1572868
  205.0 4.3 %slice-start.1 = ((s8[6291456]{0:T(1024)(128)(4,1)}), s8[2097152]{0:T(1024)(128)(4,1)S(1)}, s32[]{:S(2)}) async-start(s8[6291456]{0:T(1024)(128)(4,1)} %bitcast.60), calls=%async_computation.1 | async-start | bytes 4194304
where the time goes:
time: 213 us; the launch traced here: 212 us
  Pallas kernels  176 us (83%)
  matrix products  17.3 us (8%)
  other arithmetic  10.7 us (5%)
  local copies, waits for them, and re-layouts  7.35 us (3%)
    pallas_call x1, Pallas kernels, dispatch(): pl.pallas_call(functools.partial(dispatch_kernel, rows, cols, cap), out_s...  99.7 us
    pallas_call x1, Pallas kernels, combine(): pl.pallas_call(functools.partial(combine_kernel, rows, cols), out_shape=(...  76.1 us
    dot_general x7, matrix products, contract(): lax.dot_general(a, b, (((da,), (db,)), ((), ())), preferred_element_type=...  14.5 us
    another operation x1, other arithmetic  5.05 us

commit v1 on v0

--- a/solution.py
+++ b/solution.py
@@ -1,4 +1,5 @@
 import functools
+import math
 
 import jax
 import jax.numpy as jnp
@@ -49,7 +50,7 @@
 
 
 def dispatch_kernel(
-    rows, cols, cap,
+    rows, cols, cap, top,
     tok_ref, doc_ref, qry_ref, meta_ref, wgu_ref,
     x_ref, docs_ref, qrys_ref, metas_ref, proj_ref, dm_ref,
     tokc, packed, w, own_sem, w_sem, zs, zr, gs, gr, rs, ds, dr,
@@ -58,7 +59,6 @@
     n_tok, width = tok_ref.shape
     n_doc, w_doc = doc_ref.shape
     n_qry, w_qry = qry_ref.shape
-    top = 8
     step = width // CHUNKS
     block = cols * cap
     chips = rows // 2
@@ -221,7 +221,7 @@
             outgoing(f, s, row, lax.rem(row + s, rows)).wait_send()
 
 
-def dispatch(rows, cols, cap, tokens, documents, questions, meta, gate_up):
+def dispatch(rows, cols, cap, top, tokens, documents, questions, meta, gate_up):
     n_tok, width = tokens.shape
     n_doc, w_doc = documents.shape
     n_qry, w_qry = questions.shape
@@ -231,7 +231,7 @@
     vmem = pl.BlockSpec(memory_space=pltpu.VMEM)
     hbm = pl.BlockSpec(memory_space=pl.ANY)
     return pl.pallas_call(
-        functools.partial(dispatch_kernel, rows, cols, cap),
+        functools.partial(dispatch_kernel, rows, cols, cap, top),
         out_shape=(
             jax.ShapeDtypeStruct((slots, width), BF),
             jax.ShapeDtypeStruct((cols * n_doc, rows * w_doc), BF),
@@ -401,6 +401,563 @@
     )(pre_grad, dispatch_t, cot_tok, gate_up, slot_inputs)
 
 
+def fused_kernel(
+    rows, cols, cap, first_widths, last_widths,
+    tok_ref, doc_ref, qry_ref, pos_ref, ids_ref, rw_ref, wgu_ref, down_ref,
+    passage_ref, out_ref, gug_ref, dg_ref,
+    meta, metas, tokc, packed, x, w, down, proj, dm, dmt, place, weight, placed, group,
+    docs, qrow, qcols, dsc, cot, cot_down, spread, hgrad, hidden, pre, ret, comb, parts,
+    hbq, stage,
+    own_sem, load_sem, zs, zr, gs, gr, rs, ds, dr, qs, qr, ss, sr, es, er, fs, fr, out_sem,
+):
+    row, col = lax.axis_index("row"), lax.axis_index("col")
+    me = row * cols + col
+    n_tok, width = tok_ref.shape
+    n_doc, w_doc = doc_ref.shape
+    n_qry, w_qry = qry_ref.shape
+    top = ids_ref.shape[1]
+    ff = down.shape[0]
+    slots = x.shape[0]
+    block = slots // rows
+    pair = 2 * block
+    chips = rows // 2
+    core = lax.rem(row, 2)
+    chip = lax.div(row, 2)
+    sibling = row + 1 - 2 * core
+    line_q = cols * n_tok // SEQ_LEN
+
+    def cuts(widths):
+        edges, at = [], 0
+        for size in widths:
+            edges.append((at, size))
+            at += size
+        return edges
+
+    first, last = cuts(first_widths), cuts(last_widths)
+    n_first, n_last = len(first), len(last)
+
+    def line_piece(kind, c):
+        if kind == 0:
+            return doc_ref, docs.at[span(c, n_doc), span(row, w_doc)]
+        if kind == 1:
+            return meta, metas.at[row * cols + c]
+        if kind == 2:
+            return qry_ref, qrow.at[:, span(c, w_qry)]
+        at, size = first[kind - 3]
+        return tok_ref.at[:, pl.ds(at, size)], tokc.at[span(c, n_tok), pl.ds(at, size)]
+
+    def along_line(kind, s, origin, to):
+        src, dst = line_piece(kind, origin)
+        return remote(src, dst, zs.at[kind, s], zr.at[kind, origin], (row, to))
+
+    def own(kind):
+        src, dst = line_piece(kind, col)
+        return pltpu.make_async_copy(src, dst, own_sem.at[kind])
+
+    loads = [
+        pltpu.make_async_copy(wgu_ref.at[pl.ds(at, size)], w.at[pl.ds(at, size)], load_sem.at[f])
+        for f, (at, size) in enumerate(first)
+    ]
+    loads.append(pltpu.make_async_copy(down_ref, down, load_sem.at[n_first]))
+
+    meta[:top] = ids_ref[...].astype(F32).T
+    meta[top:] = rw_ref[...].T
+    greet(rows, cols)
+    order = [0, 1, 3, 2] + list(range(4, 3 + n_first))
+    for kind in order:
+        for s in range(1, cols):
+            along_line(kind, s, col, lax.rem(col + s, cols)).start()
+        own(kind).start()
+    for copy in loads:
+        copy.start()
+
+    def line_arrived(kind):
+        own(kind).wait()
+        for s in range(1, cols):
+            origin = lax.rem(col + s, cols)
+            along_line(kind, s, origin, origin).wait_recv()
+
+    def strip(kind, r):
+        if kind == 0:
+            return docs.at[:, span(r, w_doc)]
+        return metas.at[pl.ds(r * cols, cols)]
+
+    def peer(s):
+        return 2 * lax.rem(chip + s, chips) + core
+
+    def direct(kind, s, origin, to):
+        return remote(strip(kind, origin), strip(kind, origin), gs.at[kind, s],
+                      gr.at[kind, origin], (to, col))
+
+    def relay(kind, s, origin):
+        return remote(strip(kind, origin), strip(kind, origin), rs.at[kind, s],
+                      gr.at[kind, origin], (sibling, col))
+
+    def spread_out(kind):
+        line_arrived(kind)
+        for s in range(1, chips):
+            direct(kind, s, row, peer(s)).start()
+        direct(kind, 0, row, sibling).start()
+
+    def pass_on(kind):
+        for s in range(1, chips):
+            origin = peer(s)
+            direct(kind, s, origin, origin).wait_recv()
+            relay(kind, s, origin).start()
+
+    def all_here(kind):
+        direct(kind, 0, sibling, sibling).wait_recv()
+        for s in range(1, chips):
+            relay(kind, s, 2 * lax.rem(chip + s, chips) + 1 - core).wait_recv()
+
+    before = (
+        lax.broadcasted_iota(jnp.int32, (n_tok, n_tok), 0)
+        < lax.broadcasted_iota(jnp.int32, (n_tok, n_tok), 1)
+    ).astype(BF)
+    slot = lax.broadcasted_iota(jnp.int32, (block, n_tok), 0).astype(F32)
+
+    def outgoing(f, s, origin, to):
+        part = pl.ds(*first[f])
+        return remote(packed.at[span(to, block), part], x.at[span(origin, block), part],
+                      ds.at[f, s], dr.at[f, origin], (to, col))
+
+    def kept(f):
+        part = pl.ds(*first[f])
+        return pltpu.make_async_copy(
+            packed.at[span(row, block), part], x.at[span(row, block), part],
+            own_sem.at[3 + n_first + f],
+        )
+
+    def pack(f):
+        line_arrived(3 + f)
+        part = pl.ds(*first[f])
+
+        @pl.loop(0, chips)
+        def _(m):
+            packed[span(m, pair), part] = contract(
+                dm[span(m, pair), :], tokc[:, part], 1, 0
+            ).astype(BF)
+
+        for s in range(1, rows):
+            outgoing(f, s, row, lax.rem(row + s, rows)).start()
+        kept(f).start()
+
+    tile = 512
+
+    def project(f):
+        loads[f].wait()
+        kept(f).wait()
+        for s in range(1, rows):
+            origin = lax.rem(row + s, rows)
+            outgoing(f, s, origin, origin).wait_recv()
+        part = pl.ds(*first[f])
+
+        @pl.loop(0, 2 * ff // tile)
+        def _(n):
+            term = contract(x[:, part], w[part, span(n, tile)], 1, 0)
+            if f == 0:
+                proj[:, span(n, tile)] = term
+            else:
+                proj[:, span(n, tile)] += term
+
+    def query_piece(origin, to):
+        return qrow.at[:, span(to, w_doc)], qcols.at[span(origin, n_qry), :]
+
+    def queries(s, origin, to):
+        src, dst = query_piece(origin, to)
+        return remote(src, dst, qs.at[s], qr.at[origin], (to, col))
+
+    def own_queries():
+        src, dst = query_piece(row, row)
+        return pltpu.make_async_copy(src, dst, own_sem.at[3 + 2 * n_first])
+
+    def scored(s, origin, to):
+        rows_of = dsc.at[span(origin, n_qry), :]
+        return remote(rows_of, rows_of, ss.at[s], sr.at[origin], (to, col))
+
+    spread_out(0)
+    spread_out(1)
+    target = (
+        lax.broadcasted_iota(jnp.int32, (rows, n_tok), 0) * cols + col
+    ).astype(F32)
+    for c in range(cols):
+        ids = metas[row * cols + c, :top]
+        hit = jnp.zeros((rows, n_tok), F32)
+        for k in range(top):
+            hit = hit + (ids[k : k + 1, :] == target).astype(F32)
+        rank = contract(hit.astype(BF), before, 1, 0)
+        spot = jnp.where(hit > 0.5, rank + float(c * cap), -1.0)
+        for r in range(rows):
+            dm[r * block : (r + 1) * block, c * n_tok : (c + 1) * n_tok] = jnp.where(
+                slot == spot[r : r + 1, :], 1.0, 0.0
+            ).astype(BF)
+    pack(0)
+
+    pass_on(0)
+    pass_on(1)
+    line_arrived(2)
+    for s in range(1, rows):
+        queries(s, row, lax.rem(row + s, rows)).start()
+    own_queries().start()
+    all_here(0)
+    scores = contract(qrow[...], docs[...], 1, 1) / sharpness_divisor
+    peak = jnp.max(scores, axis=1, keepdims=True)
+    grown = jnp.exp(scores - peak)
+    total = jnp.sum(grown, axis=1, keepdims=True)
+    onehot = (
+        pos_ref[...] == lax.broadcasted_iota(jnp.int32, scores.shape, 1)
+    ).astype(F32)
+    dsc[span(row, n_qry), :] = ((grown / total - onehot) / sharpness_divisor).astype(BF)
+    for c in range(cols):
+        here = slice(c * n_tok, (c + 1) * n_tok)
+        dmt[here, :] = dm[:, here].astype(F32).T.astype(BF)
+    for s in range(1, rows):
+        scored(s, row, lax.rem(row + s, rows)).start()
+    pack(1)
+
+    all_here(1)
+    lines = rows * cols
+    each = lax.broadcasted_iota(jnp.int32, (lines, n_tok), 0)
+    mine = me.astype(F32)
+    chosen = jnp.zeros((lines, n_tok), F32)
+    amount = jnp.zeros((lines, n_tok), F32)
+    for b in range(lines):
+        hit = (metas[b, :top] == mine).astype(F32)
+        found = jnp.sum(hit, axis=0, keepdims=True)
+        value = jnp.sum(hit * metas[b, top:], axis=0, keepdims=True)
+        chosen = jnp.where(each == b, found, chosen)
+        amount = jnp.where(each == b, value, amount)
+    rank = contract(chosen.astype(BF), before, 1, 0)
+    begin = (lax.rem(each, cols) * cap).astype(F32)
+    place[...] = jnp.where(chosen > 0.5, rank + begin, -1.0)
+    weight[...] = amount
+    group[...] = (
+        lax.broadcasted_iota(jnp.int32, (cols * n_tok, line_q), 0) // SEQ_LEN
+        == lax.broadcasted_iota(jnp.int32, (cols * n_tok, line_q), 1)
+    ).astype(BF)
+
+    @pl.loop(0, rows)
+    def _(r):
+        for c in range(cols):
+            here = pl.ds(r * cols + c, 1)
+            placed[:, c * n_tok : (c + 1) * n_tok] = jnp.where(
+                slot == place[here, :], weight[here, :], 0.0
+            ).astype(BF)
+        spread[span(r, block), :] = contract(placed[...], group[...], 1, 0).astype(BF)
+
+    project(0)
+    pack(2)
+
+    for s in range(1, rows):
+        origin = lax.rem(row + s, rows)
+        scored(s, origin, origin).wait_recv()
+
+    @pl.loop(0, width // tile)
+    def _(n):
+        cot[:, span(n, tile)] = (
+            contract(dsc[...], docs[:, span(n, tile)], 1, 0) / SEQ_LEN
+        ).astype(BF)
+
+    loads[n_first].wait()
+    small = 256
+
+    @pl.loop(0, ff // small)
+    def _(n):
+        cot_down[:, span(n, small)] = contract(
+            cot[...], down[span(n, small), :], 1, 1
+        ).astype(BF)
+
+    project(1)
+    for f in range(3, n_first):
+        pack(f)
+        if f < n_first - 1 or f > 3:
+            project(f - 1)
+    for s in range(1, rows):
+        origin = lax.rem(row + s, rows)
+        queries(s, origin, origin).wait_recv()
+    own_queries().wait()
+    passage_ref[...] = contract(dsc[:, span(col, n_doc)], qcols[...], 0, 0)
+    if n_first == 4:
+        project(2)
+
+    def returning(f, s, origin, to):
+        part = pl.ds(*last[f])
+        return remote(packed.at[span(to, block), part], ret.at[span(origin, block), part],
+                      es.at[f, s], er.at[f, origin], (to, col))
+
+    def held(f):
+        part = pl.ds(*last[f])
+        return pltpu.make_async_copy(
+            packed.at[span(row, block), part], ret.at[span(row, block), part],
+            own_sem.at[4 + 2 * n_first + f],
+        )
+
+    def home(f, s, origin, to):
+        part = pl.ds(*last[f])
+        return remote(comb.at[span(to, n_tok), part], parts.at[origin, :, part],
+                      fs.at[f, s], fr.at[f, origin], (row, to))
+
+    drained = set()
+
+    def drain(g):
+        low, size = last[g]
+        for f, (at, wide) in enumerate(first):
+            if f not in drained and at < low + size and low < at + wide:
+                drained.add(f)
+                for s in range(1, rows):
+                    outgoing(f, s, row, lax.rem(row + s, rows)).wait_send()
+
+    f_end = n_first - 1
+    loads[f_end].wait()
+    kept(f_end).wait()
+    drain(0)
+    end = pl.ds(*first[f_end])
+    begin_cols = pl.ds(*last[0])
+    lane = 128
+
+    def offset_of(r):
+        return lax.rem(r - row + rows, rows)
+
+    for s in range(chips):
+        other = lax.rem(chip + s, chips)
+        two = (2 * other + core, 2 * other + 1 - core)
+        for k, origin in enumerate(two):
+            if s == 0 and k == 0:
+                continue
+            outgoing(f_end, offset_of(origin), origin, origin).wait_recv()
+        here = span(other, pair)
+
+        @pl.loop(0, 2 * ff // tile)
+        def _(n):
+            proj[here, span(n, tile)] += contract(x[here, end], w[end, span(n, tile)], 1, 0)
+
+        for k in range(2):
+            r = 2 * other + k
+            at = span(r, block)
+            hgrad[...] = contract(spread[at, :], cot_down[span(r, line_q), :], 1, 0)
+
+            @pl.loop(0, ff // lane)
+            def _(n):
+                left = span(n, lane)
+                right = pl.ds(pl.multiple_of(ff + n * lane, lane), lane)
+                gate, up = proj[at, left], proj[at, right]
+                sig = jax.nn.sigmoid(gate)
+                act = gate * sig
+                grad = hgrad[:, left]
+                hidden[at, left] = (act * up).astype(BF)
+                pre[at, left] = (grad * up * (sig * (1.0 + gate * (1.0 - sig)))).astype(BF)
+                pre[at, right] = (grad * act).astype(BF)
+
+        packed[here, begin_cols] = contract(pre[here, :], w[begin_cols, :], 1, 1).astype(BF)
+        for k, to in enumerate(two):
+            if s == 0 and k == 0:
+                held(0).start()
+            else:
+                returning(0, offset_of(to), row, to).start()
+
+    for f in range(1, n_last):
+        at, size = last[f]
+        drain(f)
+
+        @pl.loop(0, size // small)
+        def _(n):
+            part = pl.ds(pl.multiple_of(at + n * small, small), small)
+            packed[:, part] = contract(pre[...], w[part, :], 1, 1).astype(BF)
+
+        for s in range(1, rows):
+            returning(f, s, row, lax.rem(row + s, rows)).start()
+        held(f).start()
+
+    @pl.loop(0, rows)
+    def _(r):
+        hbq[span(r, line_q), :] = contract(
+            spread[span(r, block), :], hidden[span(r, block), :], 0, 0
+        ).astype(BF)
+
+    n_gate, n_down = width // small, ff // small
+
+    def gate_out(i):
+        return pltpu.make_async_copy(
+            stage.at[i % 2, :, pl.ds(0, 2 * ff)], gug_ref.at[pl.ds(i * small, small)],
+            out_sem.at[i % 2],
+        )
+
+    def down_out(i):
+        j = n_gate + i
+        return pltpu.make_async_copy(
+            stage.at[j % 2], dg_ref.at[pl.ds(i * small, small)], out_sem.at[j % 2]
+        )
+
+    def grad_out(i):
+        return gate_out(i) if i < n_gate else down_out(i - n_gate)
+
+    def grad_tile(i):
+        if i >= 2:
+            grad_out(i - 2).wait()
+        if i < n_gate:
+            stage[i % 2, :, : 2 * ff] = contract(
+                x[:, i * small : (i + 1) * small], pre[...], 0, 0
+            ).astype(BF)
+        else:
+            j = i - n_gate
+            stage[i % 2] = contract(hbq[:, j * small : (j + 1) * small], cot[...], 0, 0).astype(BF)
+        grad_out(i).start()
+
+    def merge(f):
+        held(f).wait()
+        for s in range(1, rows):
+            origin = lax.rem(row + s, rows)
+            returning(f, s, origin, origin).wait_recv()
+        part = pl.ds(*last[f])
+        comb[:, part] = contract(dmt[...], ret[:, part], 1, 0).astype(BF)
+        for s in range(1, cols):
+            home(f, s, col, lax.rem(col + s, cols)).start()
+
+    per_dev = n_tok // SEQ_LEN
+    repeat = (
+        lax.broadcasted_iota(jnp.int32, (n_tok, per_dev), 0) // SEQ_LEN
+        == lax.broadcasted_iota(jnp.int32, (n_tok, per_dev), 1)
+    ).astype(BF)
+
+    def finish(f):
+        part = pl.ds(*last[f])
+        sums = contract(repeat, cot[span(me, per_dev), part], 1, 0)
+        sums = sums + comb[span(col, n_tok), part].astype(F32)
+        for s in range(1, cols):
+            origin = lax.rem(col + s, cols)
+            home(f, s, origin, origin).wait_recv()
+            sums = sums + parts[origin, :, part].astype(F32)
+        out_ref[:, part] = sums.astype(BF)
+
+    tiles = n_gate + n_down
+    done = 0
+    for f in range(n_last):
+        merge(f)
+        if f >= 1:
+            finish(f - 1)
+        until = tiles * (f + 1) // n_last
+        for i in range(done, until):
+            grad_tile(i)
+        done = until
+    finish(n_last - 1)
+    for i in range(tiles - 2, tiles):
+        grad_out(i).wait()
+
+    for kind in range(2):
+        for s in range(1, chips):
+            direct(kind, s, row, peer(s)).wait_send()
+            relay(kind, s, peer(s)).wait_send()
+        direct(kind, 0, row, sibling).wait_send()
+    for kind in range(3 + n_first):
+        for s in range(1, cols):
+            along_line(kind, s, col, lax.rem(col + s, cols)).wait_send()
+    for s in range(1, rows):
+        to = lax.rem(row + s, rows)
+        queries(s, row, to).wait_send()
+        scored(s, row, to).wait_send()
+        for f in range(n_last):
+            returning(f, s, row, to).wait_send()
+    for f in range(n_last):
+        for s in range(1, cols):
+            home(f, s, col, lax.rem(col + s, cols)).wait_send()
+
+
+def fused_plan(rows, cols, cap, top, tokens, documents, questions, down):
+    n_tok, width = tokens.shape
+    n_doc, w_doc = documents.shape
+    n_qry = questions.shape[0]
+    ff = down.shape[0]
+    block = cols * cap
+    slots = rows * block
+    line = cols * n_tok
+    line_q = line // SEQ_LEN
+    n_all = rows * n_qry
+    stage_rows = 256
+    return [
+        ((2 * top, n_tok), F32),
+        ((rows * cols, 2 * top, n_tok), F32),
+        ((line, width), BF),
+        ((slots, width), BF),
+        ((slots, width), BF),
+        ((width, 2 * ff), BF),
+        ((ff, width), BF),
+        ((slots, 2 * ff), F32),
+        ((slots, line), BF),
+        ((line, slots), BF),
+        ((rows * cols, n_tok), F32),
+        ((rows * cols, n_tok), F32),
+        ((block, line), BF),
+        ((line, line_q), BF),
+        ((cols * n_doc, width), BF),
+        ((n_qry, width), BF),
+        ((n_all, w_doc), BF),
+        ((n_all, cols * n_doc), BF),
+        ((n_all, width), BF),
+        ((n_all, ff), BF),
+        ((slots, line_q), BF),
+        ((block, ff), F32),
+        ((slots, ff), BF),
+        ((slots, 2 * ff), BF),
+        ((slots, width), BF),
+        ((line, width), BF),
+        ((cols, n_tok, width), BF),
+        ((n_all, ff), BF),
+        ((2, stage_rows, max(width, 2 * ff)), BF),
+    ]
+
+
+def plan_bytes(plan):
+    return sum(math.prod(shape) * jnp.dtype(kind).itemsize for shape, kind in plan)
+
+
+def fused(rows, cols, cap, plan, tokens, documents, questions, positive, ids, weights, gate_up, down):
+    n_tok, width = tokens.shape
+    n_doc, w_doc = documents.shape
+    hidden2 = gate_up.shape[1]
+    first = [width // 4] * 4
+    last = [width // 4] * 3 + [width // 8] * 2
+    dma = pltpu.SemaphoreType.DMA
+    vmem = pl.BlockSpec(memory_space=pltpu.VMEM)
+    hbm = pl.BlockSpec(memory_space=pl.ANY)
+    n_first, n_last = len(first), len(last)
+    return pl.pallas_call(
+        functools.partial(fused_kernel, rows, cols, cap, first, last),
+        out_shape=(
+            jax.ShapeDtypeStruct((n_doc, w_doc), F32),
+            jax.ShapeDtypeStruct((n_tok, width), BF),
+            jax.ShapeDtypeStruct((width, hidden2), BF),
+            jax.ShapeDtypeStruct(down.shape, BF),
+        ),
+        in_specs=[vmem] * 6 + [hbm] * 2,
+        out_specs=[vmem, vmem, hbm, hbm],
+        scratch_shapes=[pltpu.VMEM(shape, kind) for shape, kind in plan]
+        + [
+            dma((4 + 2 * n_first + n_last,)),
+            dma((n_first + 1,)),
+            dma((3 + n_first, cols)),
+            dma((3 + n_first, cols)),
+            dma((2, rows)),
+            dma((2, rows)),
+            dma((2, rows)),
+            dma((n_first, rows)),
+            dma((n_first, rows)),
+            dma((rows,)),
+            dma((rows,)),
+            dma((rows,)),
+            dma((rows,)),
+            dma((n_last, rows)),
+            dma((n_last, rows)),
+            dma((n_last, cols)),
+            dma((n_last, cols)),
+            dma((2,)),
+        ],
+        compiler_params=pltpu.CompilerParams(
+            collective_id=2, has_side_effects=True, vmem_limit_bytes=VMEM_LIMIT
+        ),
+        name="fused",
+    )(tokens, documents, questions, positive[:, None], ids, weights, gate_up, down)
+
+
 def shards(
     question_vectors,
     document_vectors,
@@ -426,12 +983,20 @@
     gate_up = expert_gate_up[0]
     down = expert_down[0]
 
+    plan = fused_plan(rows, cols, cap, top, tokens, document_vectors, question_vectors, down)
+    if plan_bytes(plan) < VMEM_LIMIT - 6_000_000:
+        passage_grad, token_grad, gate_up_grad, down_grad = fused(
+            rows, cols, cap, plan, tokens, document_vectors, question_vectors, positive,
+            expert_ids, route_weights, gate_up, down,
+        )
+        return (passage_grad, token_grad, gate_up_grad[None], down_grad[None])
+
     n_qry = positive.shape[0]
     pos_rows = -(-n_qry // (8 * LANES)) * 8
     pos = jnp.pad(positive, (0, pos_rows * LANES - n_qry)).astype(F32).reshape(pos_rows, LANES)
     meta = jnp.concatenate([expert_ids.T.astype(F32), route_weights.T, pos], axis=0)
     slot_inputs, docs, qrys, metas, projected, dm = dispatch(
-        rows, cols, cap, tokens, document_vectors, question_vectors, meta, gate_up
+        rows, cols, cap, top, tokens, document_vectors, question_vectors, meta, gate_up
     )
 
     ids = metas[:, :top].astype(jnp.int32)

time: 213 us -> 185 us (0.87)
  matrix products: 17.3 us -> 0 us
  other arithmetic: 10.7 us -> 0 us
  local copies, waits for them, and re-layouts: 7.35 us -> 15.4 us
  Pallas kernels: 176 us -> 169 us
    dot_general x9 -> x0, matrix products: 17.3 us -> none  [the longest x7 14.5 us: contract(): lax.dot_general(a, b, (((da,), (db,)), ((), ())), preferred_element_type=...]
    unnamed x22 -> x8, local copies, waits for them, and re-layouts: 3.63 us -> 14 us
    pallas_call x2 -> x1, Pallas kernels: 176 us -> 169 us  [fused(): pl.pallas_call(functools.partial(fused_kernel, rows, cols, cap, first, la...]
    another operation x1 -> x0, other arithmetic: 5.05 us -> none
    concatenate x2 -> x0, other arithmetic: 3.36 us -> none  [the longest x1 2.07 us: shards(): jnp.concatenate([hidden_grad * up_part * slope, hidden_grad * activated],...]
where the time goes in v1:
time: 185 us
  Pallas kernels  169 us (91%)
  local copies, waits for them, and re-layouts  15.4 us (8%)
    pallas_call x1, Pallas kernels, fused(): pl.pallas_call(functools.partial(fused_kernel, rows, cols, cap, first, la...  169 us
    unnamed x8, local copies, waits for them, and re-layouts  14 us

profile of v1, /device:TPU:0, one launch (start us, length us, event | category | flops | bytes accessed | tf_op | source)
XLA Modules:
  0.0 184.8 jit_solution(7654383744194601363)
XLA Ops:
  0.6 1.4 copy.12.pos_ref
  2.0 1.4 copy.13.ids_ref
  3.4 1.4 copy.14.rw_ref
  4.8 168.8 %fused.1 = (f32[128,256]{1,0:T(8,128)}, bf16[128,2048]{1,0:T(8,128)(2,1)}, bf16[2048,1536]{1,0:T(8,128)(2,1)}, bf16[768,2048]{1,0:T(8,128)(2,1)}) custom-call(bf16[128,2048]{1,0:T(8,128)(2,1)} %tok_ref.1, bf16[128,256]{1,0:T(8,128)(2,1)} %doc_ref.1, bf16[64,512]{1,0:T(8,128)(2,1)} %qry_ref.1, s32[64,1]{1,0:T(8,128)} %copy.12.pos_ref, ...), custom_call_target="tpu_custom_call" | custom-call | tf_op jit(solution)/shard_map/fused/pallas_call | solution.py:923
  173.6 1.6 copy.19
  175.2 1.9 %copy.20 = bf16[128,2048]{1,0:T(8,128)(2,1)} copy(bf16[128,2048]{1,0:T(8,128)(2,1)} %get-tuple-element.17) | data formatting | bytes 1048576
  177.1 0.0 copy-start
  177.1 6.0 %copy.21 = bf16[1,2048,1536]{2,1,0:T(8,128)(2,1)} copy(bf16[1,2048,1536]{2,1,0:T(8,128)(2,1)} %bitcast.6) | data formatting | bytes 12582912
  183.1 0.0 copy-done
  183.1 1.7 copy.22
Async XLA Ops:
  177.1 6.1 %copy-start = (bf16[768,2048]{1,0:T(8,128)(2,1)S(1)}, bf16[768,2048]{1,0:T(8,128)(2,1)}, u32[]{:S(2)}) copy-start(bf16[768,2048]{1,0:T(8,128)(2,1)} %get-tuple-element.11) | copy-start | bytes 9437188

commit v2 on v1

--- a/solution.py
+++ b/solution.py
@@ -415,7 +415,7 @@
     n_tok, width = tok_ref.shape
     n_doc, w_doc = doc_ref.shape
     n_qry, w_qry = qry_ref.shape
-    top = ids_ref.shape[1]
+    top = ids_ref.shape[0]
     ff = down.shape[0]
     slots = x.shape[0]
     block = slots // rows
@@ -424,6 +424,16 @@
     core = lax.rem(row, 2)
     chip = lax.div(row, 2)
     sibling = row + 1 - 2 * core
+
+    def flip(index, k, count):
+        total, bit = 0, 1
+        while bit < count:
+            digit = lax.rem(lax.div(index, bit), 2)
+            total = total + bit * (1 - digit if k & bit else digit)
+            bit *= 2
+        return total
+
+    mates = list(range(2, rows)) + [1]
     line_q = cols * n_tok // SEQ_LEN
 
     def cuts(widths):
@@ -446,9 +456,39 @@
         at, size = first[kind - 3]
         return tok_ref.at[:, pl.ds(at, size)], tokc.at[span(c, n_tok), pl.ds(at, size)]
 
-    def along_line(kind, s, origin, to):
-        src, dst = line_piece(kind, origin)
-        return remote(src, dst, zs.at[kind, s], zr.at[kind, origin], (row, to))
+    ways = ((0, 1), (1, -1))
+
+    def can_send(way):
+        return col < cols - 1 if way == 0 else col > 0
+
+    def hop(kind, step, way, block, to):
+        src, dst = line_piece(kind, block)
+        return remote(src if step == 0 else dst, dst, zs.at[kind, way, step],
+                      zr.at[kind, block], (row, to))
+
+    def advance(kinds, step):
+        for kind in kinds:
+            for way, d in ways:
+                origin = col - d * step
+                came = origin >= 0 if way == 0 else origin < cols
+                if step:
+                    @pl.when(came)
+                    def _():
+                        hop(kind, step, way, origin, col).wait_recv()
+
+                @pl.when(jnp.logical_and(came, can_send(way)))
+                def _():
+                    hop(kind, step, way, origin, col + d).start()
+
+    def settle(kind):
+        for step in range(cols):
+            for way, d in ways:
+                origin = col - d * step
+                came = origin >= 0 if way == 0 else origin < cols
+
+                @pl.when(jnp.logical_and(came, can_send(way)))
+                def _():
+                    hop(kind, step, way, origin, col + d).wait_send()
 
     def own(kind):
         src, dst = line_piece(kind, col)
@@ -460,22 +500,24 @@
     ]
     loads.append(pltpu.make_async_copy(down_ref, down, load_sem.at[n_first]))
 
-    meta[:top] = ids_ref[...].astype(F32).T
-    meta[top:] = rw_ref[...].T
+    meta[:top] = ids_ref[...].astype(F32)
+    meta[top:] = rw_ref[...]
+    for kind in range(3 + n_first):
+        own(kind).start()
     greet(rows, cols)
-    order = [0, 1, 3, 2] + list(range(4, 3 + n_first))
-    for kind in order:
-        for s in range(1, cols):
-            along_line(kind, s, col, lax.rem(col + s, cols)).start()
-        own(kind).start()
+    queue = [(0, 1), (3,), (4,), (2,)] + [(kind,) for kind in range(5, 3 + n_first)]
+    advance(queue[0], 0)
+    advance(queue[1], 0)
     for copy in loads:
         copy.start()
 
-    def line_arrived(kind):
-        own(kind).wait()
-        for s in range(1, cols):
-            origin = lax.rem(col + s, cols)
-            along_line(kind, s, origin, origin).wait_recv()
+    def gathered(i):
+        for step in range(1, cols):
+            advance(queue[i], step)
+        for kind in queue[i]:
+            own(kind).wait()
+        if i + 2 < len(queue):
+            advance(queue[i + 2], 0)
 
     def strip(kind, r):
         if kind == 0:
@@ -483,7 +525,7 @@
         return metas.at[pl.ds(r * cols, cols)]
 
     def peer(s):
-        return 2 * lax.rem(chip + s, chips) + core
+        return 2 * flip(chip, s, chips) + core
 
     def direct(kind, s, origin, to):
         return remote(strip(kind, origin), strip(kind, origin), gs.at[kind, s],
@@ -494,7 +536,6 @@
                       gr.at[kind, origin], (sibling, col))
 
     def spread_out(kind):
-        line_arrived(kind)
         for s in range(1, chips):
             direct(kind, s, row, peer(s)).start()
         direct(kind, 0, row, sibling).start()
@@ -508,7 +549,7 @@
     def all_here(kind):
         direct(kind, 0, sibling, sibling).wait_recv()
         for s in range(1, chips):
-            relay(kind, s, 2 * lax.rem(chip + s, chips) + 1 - core).wait_recv()
+            relay(kind, s, peer(s) + 1 - 2 * core).wait_recv()
 
     before = (
         lax.broadcasted_iota(jnp.int32, (n_tok, n_tok), 0)
@@ -528,8 +569,19 @@
             own_sem.at[3 + n_first + f],
         )
 
+    def send(f, offsets):
+        for s in offsets:
+            outgoing(f, s, row, flip(row, s, rows)).start()
+
+    def sent(f, offsets):
+        for s in offsets:
+            outgoing(f, s, row, flip(row, s, rows)).wait_send()
+
+    near = tuple(k for k in mates if k < 6)
+    far = tuple(k for k in mates if k >= 6)
+    final = n_first - 1
+
     def pack(f):
-        line_arrived(3 + f)
         part = pl.ds(*first[f])
 
         @pl.loop(0, chips)
@@ -538,8 +590,6 @@
                 dm[span(m, pair), :], tokc[:, part], 1, 0
             ).astype(BF)
 
-        for s in range(1, rows):
-            outgoing(f, s, row, lax.rem(row + s, rows)).start()
         kept(f).start()
 
     tile = 512
@@ -548,7 +598,7 @@
         loads[f].wait()
         kept(f).wait()
         for s in range(1, rows):
-            origin = lax.rem(row + s, rows)
+            origin = flip(row, s, rows)
             outgoing(f, s, origin, origin).wait_recv()
         part = pl.ds(*first[f])
 
@@ -575,6 +625,7 @@
         rows_of = dsc.at[span(origin, n_qry), :]
         return remote(rows_of, rows_of, ss.at[s], sr.at[origin], (to, col))
 
+    gathered(0)
     spread_out(0)
     spread_out(1)
     target = (
@@ -591,29 +642,44 @@
             dm[r * block : (r + 1) * block, c * n_tok : (c + 1) * n_tok] = jnp.where(
                 slot == spot[r : r + 1, :], 1.0, 0.0
             ).astype(BF)
+    gathered(1)
     pack(0)
-
+    send(0, mates)
+    gathered(2)
+    pack(1)
+    for kind in range(2):
+        for s in range(1, chips):
+            direct(kind, s, row, peer(s)).wait_send()
+    send(1, mates)
     pass_on(0)
     pass_on(1)
-    line_arrived(2)
-    for s in range(1, rows):
-        queries(s, row, lax.rem(row + s, rows)).start()
+    gathered(3)
+    for s in mates:
+        queries(s, row, flip(row, s, rows)).start()
     own_queries().start()
     all_here(0)
     scores = contract(qrow[...], docs[...], 1, 1) / sharpness_divisor
     peak = jnp.max(scores, axis=1, keepdims=True)
     grown = jnp.exp(scores - peak)
     total = jnp.sum(grown, axis=1, keepdims=True)
+    square = (n_qry, n_qry)
+    diagonal = lax.broadcasted_iota(jnp.int32, square, 0) == lax.broadcasted_iota(jnp.int32, square, 1)
+    wanted = jnp.sum(
+        jnp.where(diagonal, pos_ref[...].astype(F32), 0.0), axis=1, keepdims=True
+    )
     onehot = (
-        pos_ref[...] == lax.broadcasted_iota(jnp.int32, scores.shape, 1)
+        wanted == lax.broadcasted_iota(jnp.int32, scores.shape, 1).astype(F32)
     ).astype(F32)
     dsc[span(row, n_qry), :] = ((grown / total - onehot) / sharpness_divisor).astype(BF)
     for c in range(cols):
         here = slice(c * n_tok, (c + 1) * n_tok)
         dmt[here, :] = dm[:, here].astype(F32).T.astype(BF)
-    for s in range(1, rows):
-        scored(s, row, lax.rem(row + s, rows)).start()
-    pack(1)
+    gathered(4)
+    pack(2)
+    for s in mates:
+        scored(s, row, flip(row, s, rows)).start()
+    sent(0, mates)
+    send(2, mates)
 
     all_here(1)
     lines = rows * cols
@@ -645,11 +711,14 @@
             ).astype(BF)
         spread[span(r, block), :] = contract(placed[...], group[...], 1, 0).astype(BF)
 
+    gathered(5)
+    pack(3)
     project(0)
-    pack(2)
-
-    for s in range(1, rows):
-        origin = lax.rem(row + s, rows)
+    sent(1, mates)
+    send(3, near)
+    project(1)
+    for s in mates:
+        origin = flip(row, s, rows)
         scored(s, origin, origin).wait_recv()
 
     @pl.loop(0, width // tile)
@@ -667,18 +736,14 @@
             cot[...], down[span(n, small), :], 1, 1
         ).astype(BF)
 
-    project(1)
-    for f in range(3, n_first):
-        pack(f)
-        if f < n_first - 1 or f > 3:
-            project(f - 1)
-    for s in range(1, rows):
-        origin = lax.rem(row + s, rows)
+    for s in mates:
+        origin = flip(row, s, rows)
         queries(s, origin, origin).wait_recv()
     own_queries().wait()
     passage_ref[...] = contract(dsc[:, span(col, n_doc)], qcols[...], 0, 0)
-    if n_first == 4:
-        project(2)
+    sent(2, mates)
+    send(3, far)
+    project(2)
 
     def returning(f, s, origin, to):
         part = pl.ds(*last[f])
@@ -697,34 +762,19 @@
         return remote(comb.at[span(to, n_tok), part], parts.at[origin, :, part],
                       fs.at[f, s], fr.at[f, origin], (row, to))
 
-    drained = set()
-
-    def drain(g):
-        low, size = last[g]
-        for f, (at, wide) in enumerate(first):
-            if f not in drained and at < low + size and low < at + wide:
-                drained.add(f)
-                for s in range(1, rows):
-                    outgoing(f, s, row, lax.rem(row + s, rows)).wait_send()
-
     f_end = n_first - 1
     loads[f_end].wait()
     kept(f_end).wait()
-    drain(0)
     end = pl.ds(*first[f_end])
     begin_cols = pl.ds(*last[0])
     lane = 128
 
-    def offset_of(r):
-        return lax.rem(r - row + rows, rows)
-
     for s in range(chips):
-        other = lax.rem(chip + s, chips)
-        two = (2 * other + core, 2 * other + 1 - core)
-        for k, origin in enumerate(two):
-            if s == 0 and k == 0:
-                continue
-            outgoing(f_end, offset_of(origin), origin, origin).wait_recv()
+        other = flip(chip, s, chips)
+        for k in (2 * s, 2 * s + 1):
+            if k:
+                origin = flip(row, k, rows)
+                outgoing(f_end, k, origin, origin).wait_recv()
         here = span(other, pair)
 
         @pl.loop(0, 2 * ff // tile)
@@ -749,23 +799,27 @@
                 pre[at, right] = (grad * act).astype(BF)
 
         packed[here, begin_cols] = contract(pre[here, :], w[begin_cols, :], 1, 1).astype(BF)
-        for k, to in enumerate(two):
-            if s == 0 and k == 0:
+        for k in (2 * s, 2 * s + 1):
+            if k:
+                returning(0, k, row, flip(row, k, rows)).start()
+            else:
                 held(0).start()
-            else:
-                returning(0, offset_of(to), row, to).start()
-
+
+    flushed = False
     for f in range(1, n_last):
         at, size = last[f]
-        drain(f)
-
-        @pl.loop(0, size // small)
+        if at + size > first[final][0] and not flushed:
+            flushed = True
+            sent(final, near + far)
+        bit = math.gcd(size, small)
+
+        @pl.loop(0, size // bit)
         def _(n):
-            part = pl.ds(pl.multiple_of(at + n * small, small), small)
+            part = pl.ds(pl.multiple_of(at + n * bit, bit), bit)
             packed[:, part] = contract(pre[...], w[part, :], 1, 1).astype(BF)
 
-        for s in range(1, rows):
-            returning(f, s, row, lax.rem(row + s, rows)).start()
+        for s in mates:
+            returning(f, s, row, flip(row, s, rows)).start()
         held(f).start()
 
     @pl.loop(0, rows)
@@ -806,7 +860,7 @@
     def merge(f):
         held(f).wait()
         for s in range(1, rows):
-            origin = lax.rem(row + s, rows)
+            origin = flip(row, s, rows)
             returning(f, s, origin, origin).wait_recv()
         part = pl.ds(*last[f])
         comb[:, part] = contract(dmt[...], ret[:, part], 1, 0).astype(BF)
@@ -835,7 +889,18 @@
         merge(f)
         if f >= 1:
             finish(f - 1)
-        until = tiles * (f + 1) // n_last
+        if f == 0:
+            for kind in range(2):
+                for s in range(1, chips):
+                    relay(kind, s, peer(s)).wait_send()
+                direct(kind, 0, row, sibling).wait_send()
+            for kind in range(3 + n_first):
+                settle(kind)
+            for s in mates:
+                to = flip(row, s, rows)
+                queries(s, row, to).wait_send()
+                scored(s, row, to).wait_send()
+        until = min(tiles, -(-tiles * (f + 1) // 3))
         for i in range(done, until):
             grad_tile(i)
         done = until
@@ -843,20 +908,9 @@
     for i in range(tiles - 2, tiles):
         grad_out(i).wait()
 
-    for kind in range(2):
-        for s in range(1, chips):
-            direct(kind, s, row, peer(s)).wait_send()
-            relay(kind, s, peer(s)).wait_send()
-        direct(kind, 0, row, sibling).wait_send()
-    for kind in range(3 + n_first):
-        for s in range(1, cols):
-            along_line(kind, s, col, lax.rem(col + s, cols)).wait_send()
-    for s in range(1, rows):
-        to = lax.rem(row + s, rows)
-        queries(s, row, to).wait_send()
-        scored(s, row, to).wait_send()
-        for f in range(n_last):
-            returning(f, s, row, to).wait_send()
+    for f in range(n_last):
+        for s in mates:
+            returning(f, s, row, flip(row, s, rows)).wait_send()
     for f in range(n_last):
         for s in range(1, cols):
             home(f, s, col, lax.rem(col + s, cols)).wait_send()
@@ -934,7 +988,7 @@
         + [
             dma((4 + 2 * n_first + n_last,)),
             dma((n_first + 1,)),
-            dma((3 + n_first, cols)),
+            dma((3 + n_first, 2, cols)),
             dma((3 + n_first, cols)),
             dma((2, rows)),
             dma((2, rows)),
@@ -955,7 +1009,50 @@
             collective_id=2, has_side_effects=True, vmem_limit_bytes=VMEM_LIMIT
         ),
         name="fused",
-    )(tokens, documents, questions, positive[:, None], ids, weights, gate_up, down)
+    )(tokens, documents, questions, positive.reshape(1, -1), ids.T, weights.T, gate_up, down)
+
+
+def settle_kernel(pieces, *refs):
+    count = len(pieces)
+    sources, targets = refs[:count], refs[count : 2 * count]
+    buffers, in_sem, out_sem = refs[2 * count : 3 * count], refs[-2], refs[-1]
+    todo = []
+    for i, parts in enumerate(pieces):
+        size = sources[i].shape[0] // parts
+        for p in range(parts):
+            todo.append((i, pl.ds(p * size, size)))
+    ins = [
+        pltpu.make_async_copy(sources[i].at[at], buffers[i].at[at], in_sem.at[n])
+        for n, (i, at) in enumerate(todo)
+    ]
+    outs = [
+        pltpu.make_async_copy(buffers[i].at[at], targets[i].at[at], out_sem.at[n])
+        for n, (i, at) in enumerate(todo)
+    ]
+    for copy in ins:
+        copy.start()
+    for arrived, leave in zip(ins, outs):
+        arrived.wait()
+        leave.start()
+    for copy in outs:
+        copy.wait()
+
+
+def settled(*arrays):
+    halves = [a.size * a.dtype.itemsize // (1 << 19) for a in arrays]
+    pieces = [1 << max(0, n.bit_length() - 1) for n in halves]
+    dma = pltpu.SemaphoreType.DMA
+    hbm = pl.BlockSpec(memory_space=pl.ANY)
+    return pl.pallas_call(
+        functools.partial(settle_kernel, pieces),
+        out_shape=tuple(jax.ShapeDtypeStruct(a.shape, a.dtype) for a in arrays),
+        in_specs=[hbm] * len(arrays),
+        out_specs=[hbm] * len(arrays),
+        scratch_shapes=[pltpu.VMEM(a.shape, a.dtype) for a in arrays]
+        + [dma((sum(pieces),)), dma((sum(pieces),))],
+        compiler_params=pltpu.CompilerParams(vmem_limit_bytes=VMEM_LIMIT),
+        name="settle",
+    )(*arrays)
 
 
 def shards(
@@ -984,10 +1081,13 @@
     down = expert_down[0]
 
     plan = fused_plan(rows, cols, cap, top, tokens, document_vectors, question_vectors, down)
-    if plan_bytes(plan) < VMEM_LIMIT - 6_000_000:
+    if rows == 8 and plan_bytes(plan) < VMEM_LIMIT - 6_000_000:
         passage_grad, token_grad, gate_up_grad, down_grad = fused(
             rows, cols, cap, plan, tokens, document_vectors, question_vectors, positive,
             expert_ids, route_weights, gate_up, down,
+        )
+        passage_grad, token_grad, gate_up_grad, down_grad = settled(
+            passage_grad, token_grad, gate_up_grad, down_grad
         )
         return (passage_grad, token_grad, gate_up_grad[None], down_grad[None])
 

time: 185 us -> 164 us (0.89)
  local copies, waits for them, and re-layouts: 15.4 us -> 0 us
  Pallas kernels: 169 us -> 163 us
    unnamed x8 -> x0, local copies, waits for them, and re-layouts: 14 us -> none
    pallas_call x1, Pallas kernels: 169 us -> 155 us  [fused(): pl.pallas_call(functools.partial(fused_kernel, rows, cols, cap, first, la...]
    pallas_call x0 -> x1, Pallas kernels: none -> 7.75 us  [settled(): pl.pallas_call(functools.partial(settle_kernel, pieces), out_shape=tuple(...]
where the time goes in v2:
time: 164 us; the launch traced here: 163 us
  Pallas kernels  163 us (99%)
    pallas_call x1, Pallas kernels, fused(): pl.pallas_call(functools.partial(fused_kernel, rows, cols, cap, first, la...  155 us
    pallas_call x1, Pallas kernels, settled(): pl.pallas_call(functools.partial(settle_kernel, pieces), out_shape=tuple(...  7.75 us

profile of v2, /device:TPU:0, one launch (start us, length us, event | category | flops | bytes accessed | tf_op | source)
XLA Modules:
  0.0 163.4 jit_solution(16254574227066919050)
XLA Ops:
  0.6 154.9 %fused.1 = (f32[128,256]{1,0:T(8,128)}, bf16[128,2048]{1,0:T(8,128)(2,1)}, bf16[2048,1536]{1,0:T(8,128)(2,1)}, bf16[768,2048]{1,0:T(8,128)(2,1)}) custom-call(bf16[128,2048]{1,0:T(8,128)(2,1)} %tok_ref.1, bf16[128,256]{1,0:T(8,128)(2,1)} %doc_ref.1, bf16[64,512]{1,0:T(8,128)(2,1)} %qry_ref.1, s32[1,64]{1,0:T(1,128)} %bitcast.11, s32[8,128]{1,0:T(8,128)} %bitcast.9, ...), custom_call_target="tpu_custom_call" | custom-call | tf_op jit(solution)/shard_map/fused/pallas_call | solution.py:977
  155.5 7.7 %settle.1 = (f32[128,256]{1,0:T(8,128)}, bf16[128,2048]{1,0:T(8,128)(2,1)}, bf16[2048,1536]{1,0:T(8,128)(2,1)}, bf16[768,2048]{1,0:T(8,128)(2,1)}) custom-call(f32[128,256]{1,0:T(8,128)} %get-tuple-element.12.refs_0_, bf16[128,2048]{1,0:T(8,128)(2,1)} %get-tuple-element.13.refs_1_, bf16[2048,1536]{1,0:T(8,128)(2,1)} %get-tuple-element.14.refs_2_, ...), custom_call_target="tpu_custom_call" | custom-call | tf_op jit(solution)/shard_map/settle/pallas_call | solution.py:1046

commit v3 on v2

--- a/solution.py
+++ b/solution.py
@@ -402,13 +402,14 @@
 
 
 def fused_kernel(
-    rows, cols, cap, first_widths, last_widths,
+    rows, cols, cap, first_widths, plane_width, last_widths,
     tok_ref, doc_ref, qry_ref, pos_ref, ids_ref, rw_ref, wgu_ref, down_ref,
     passage_ref, out_ref, gug_ref, dg_ref,
     meta, metas, tokc, packed, x, w, down, proj, dm, dmt, place, weight, placed, group,
     docs, qrow, qcols, dsc, cot, cot_down, spread, hgrad, hidden, pre, ret, comb, parts,
-    hbq, stage,
-    own_sem, load_sem, zs, zr, gs, gr, rs, ds, dr, qs, qr, ss, sr, es, er, fs, fr, out_sem,
+    hbq, stage, plane, drops, sums_out,
+    own_sem, load_sem, zs, zr, gs, gr, rs, ds, dr, qs, qr, ps, pr, es, er, fs, fr, out_sem,
+    leave_sem,
 ):
     row, col = lax.axis_index("row"), lax.axis_index("col")
     me = row * cols + col
@@ -463,7 +464,7 @@
 
     def hop(kind, step, way, block, to):
         src, dst = line_piece(kind, block)
-        return remote(src if step == 0 else dst, dst, zs.at[kind, way, step],
+        return remote(src if step == 0 else dst, dst, zs.at[kind, way],
                       zr.at[kind, block], (row, to))
 
     def advance(kinds, step):
@@ -476,29 +477,31 @@
                     def _():
                         hop(kind, step, way, origin, col).wait_recv()
 
+                    @pl.when(jnp.logical_and(came, can_send(way)))
+                    def _():
+                        hop(kind, step - 1, way, col, col + d).wait_send()
+
                 @pl.when(jnp.logical_and(came, can_send(way)))
                 def _():
                     hop(kind, step, way, origin, col + d).start()
 
     def settle(kind):
-        for step in range(cols):
-            for way, d in ways:
-                origin = col - d * step
-                came = origin >= 0 if way == 0 else origin < cols
-
-                @pl.when(jnp.logical_and(came, can_send(way)))
-                def _():
-                    hop(kind, step, way, origin, col + d).wait_send()
+        for way, d in ways:
+            @pl.when(can_send(way))
+            def _():
+                hop(kind, 0, way, col, col + d).wait_send()
 
     def own(kind):
         src, dst = line_piece(kind, col)
         return pltpu.make_async_copy(src, dst, own_sem.at[kind])
 
+    plane_cut = (sum(first_widths), plane_width)
+    plane_cols = pl.ds(*plane_cut)
     loads = [
         pltpu.make_async_copy(wgu_ref.at[pl.ds(at, size)], w.at[pl.ds(at, size)], load_sem.at[f])
-        for f, (at, size) in enumerate(first)
+        for f, (at, size) in enumerate(first + [plane_cut])
     ]
-    loads.append(pltpu.make_async_copy(down_ref, down, load_sem.at[n_first]))
+    loads.append(pltpu.make_async_copy(down_ref, down, load_sem.at[n_first + 1]))
 
     meta[:top] = ids_ref[...].astype(F32)
     meta[top:] = rw_ref[...]
@@ -508,8 +511,6 @@
     queue = [(0, 1), (3,), (4,), (2,)] + [(kind,) for kind in range(5, 3 + n_first)]
     advance(queue[0], 0)
     advance(queue[1], 0)
-    for copy in loads:
-        copy.start()
 
     def gathered(i):
         for step in range(1, cols):
@@ -522,18 +523,33 @@
     def strip(kind, r):
         if kind == 0:
             return docs.at[:, span(r, w_doc)]
-        return metas.at[pl.ds(r * cols, cols)]
+        if kind == 1:
+            return metas.at[pl.ds(r * cols, cols)]
+        if kind == 2:
+            return plane.at[span(r, n_tok), :]
+        return dsc.at[span(r, n_qry), :]
 
     def peer(s):
         return 2 * flip(chip, s, chips) + core
 
     def direct(kind, s, origin, to):
-        return remote(strip(kind, origin), strip(kind, origin), gs.at[kind, s],
-                      gr.at[kind, origin], (to, col))
-
-    def relay(kind, s, origin):
-        return remote(strip(kind, origin), strip(kind, origin), rs.at[kind, s],
-                      gr.at[kind, origin], (sibling, col))
+        src = tok_ref.at[:, plane_cols] if kind == 2 else strip(kind, origin)
+        return remote(src, strip(kind, origin), gs.at[kind], gr.at[kind, 0 if s else 1], (to, col))
+
+    def relay(kind, origin):
+        return remote(strip(kind, origin), strip(kind, origin), rs.at[kind], gr.at[kind, 1],
+                      (sibling, col))
+
+    def several(kind, count, send_sem, recv_sem):
+        if kind == 0:
+            part = docs.at[:, pl.ds(0, count * w_doc)]
+        elif kind == 1:
+            part = metas.at[pl.ds(0, count * cols)]
+        elif kind == 2:
+            part = plane.at[pl.ds(0, count * n_tok), :]
+        else:
+            part = dsc.at[pl.ds(0, count * n_qry), :]
+        return remote(part, part, send_sem, recv_sem, (sibling, col))
 
     def spread_out(kind):
         for s in range(1, chips):
@@ -541,15 +557,26 @@
         direct(kind, 0, row, sibling).start()
 
     def pass_on(kind):
+        several(kind, chips - 1, rs.at[kind], gr.at[kind, 0]).wait_recv()
         for s in range(1, chips):
-            origin = peer(s)
-            direct(kind, s, origin, origin).wait_recv()
-            relay(kind, s, origin).start()
+            relay(kind, peer(s)).start()
 
     def all_here(kind):
-        direct(kind, 0, sibling, sibling).wait_recv()
-        for s in range(1, chips):
-            relay(kind, s, peer(s) + 1 - 2 * core).wait_recv()
+        several(kind, chips, rs.at[kind], gr.at[kind, 1]).wait_recv()
+
+    def all_out(kind):
+        several(kind, chips, gs.at[kind], gr.at[kind, 0]).wait_send()
+
+    def passed(kind):
+        several(kind, chips - 1, rs.at[kind], gr.at[kind, 1]).wait_send()
+
+    own_plane = pltpu.make_async_copy(
+        tok_ref.at[:, plane_cols], strip(2, row), own_sem.at[4 + 2 * n_first + n_last]
+    )
+    spread_out(2)
+    own_plane.start()
+    for copy in loads:
+        copy.start()
 
     before = (
         lax.broadcasted_iota(jnp.int32, (n_tok, n_tok), 0)
@@ -557,10 +584,30 @@
     ).astype(BF)
     slot = lax.broadcasted_iota(jnp.int32, (block, n_tok), 0).astype(F32)
 
-    def outgoing(f, s, origin, to):
+    near = tuple(k for k in mates if k < 6)
+    far = tuple(k for k in mates if k >= 6)
+    final = n_first - 1
+
+    def outgoing(f, k, origin, to):
         part = pl.ds(*first[f])
-        return remote(packed.at[span(to, block), part], x.at[span(origin, block), part],
-                      ds.at[f, s], dr.at[f, origin], (to, col))
+        late = f == final
+        return remote(
+            packed.at[span(to, block), part], x.at[span(origin, block), part],
+            ds.at[f + 1 if late and k in far else f], dr.at[f + k // 2 if late else f], (to, col),
+        )
+
+    def batch(f, count, send_sem, recv_sem):
+        part = pl.ds(*first[f])
+        here = pl.ds(0, count * block)
+        return remote(packed.at[here, part], x.at[here, part], send_sem, recv_sem, (row, col))
+
+    def sent(f, late=False):
+        if f < final:
+            batch(f, rows - 1, ds.at[f], dr.at[f]).wait_send()
+        elif late:
+            batch(f, len(far), ds.at[f + 1], dr.at[f]).wait_send()
+        else:
+            batch(f, len(near), ds.at[f], dr.at[f]).wait_send()
 
     def kept(f):
         part = pl.ds(*first[f])
@@ -573,14 +620,6 @@
         for s in offsets:
             outgoing(f, s, row, flip(row, s, rows)).start()
 
-    def sent(f, offsets):
-        for s in offsets:
-            outgoing(f, s, row, flip(row, s, rows)).wait_send()
-
-    near = tuple(k for k in mates if k < 6)
-    far = tuple(k for k in mates if k >= 6)
-    final = n_first - 1
-
     def pack(f):
         part = pl.ds(*first[f])
 
@@ -597,9 +636,7 @@
     def project(f):
         loads[f].wait()
         kept(f).wait()
-        for s in range(1, rows):
-            origin = flip(row, s, rows)
-            outgoing(f, s, origin, origin).wait_recv()
+        batch(f, rows - 1, ds.at[f], dr.at[f]).wait_recv()
         part = pl.ds(*first[f])
 
         @pl.loop(0, 2 * ff // tile)
@@ -615,15 +652,82 @@
 
     def queries(s, origin, to):
         src, dst = query_piece(origin, to)
-        return remote(src, dst, qs.at[s], qr.at[origin], (to, col))
+        return remote(src, dst, qs.at[0], qr.at[0], (to, col))
+
+    def all_queries():
+        part = qcols.at[pl.ds(0, (rows - 1) * n_qry), :]
+        return remote(part, part, qs.at[0], qr.at[0], (sibling, col))
 
     def own_queries():
         src, dst = query_piece(row, row)
         return pltpu.make_async_copy(src, dst, own_sem.at[3 + 2 * n_first])
 
-    def scored(s, origin, to):
-        rows_of = dsc.at[span(origin, n_qry), :]
-        return remote(rows_of, rows_of, ss.at[s], sr.at[origin], (to, col))
+    share = rows * cap
+
+    def dropped(s, origin, to):
+        return remote(packed.at[span(to, share), plane_cols], drops.at[span(origin, share), :],
+                      ps.at[0], pr.at[0], (row, to))
+
+    def all_dropped():
+        part = drops.at[pl.ds(0, (cols - 1) * share), :]
+        return remote(part, part, ps.at[0], pr.at[0], (row, col))
+
+    def own_drop():
+        return pltpu.make_async_copy(
+            packed.at[span(col, share), plane_cols], drops.at[span(col, share), :],
+            own_sem.at[5 + 2 * n_first + n_last],
+        )
+
+    def pack_plane():
+        wanted_by = (
+            lax.broadcasted_iota(jnp.int32, (cols, n_tok), 0) + row * cols
+        ).astype(F32)
+        spots = lax.broadcasted_iota(jnp.int32, (share, n_tok), 0).astype(F32)
+        for r in range(rows):
+            ids = metas[r * cols + col, :top]
+            hit = jnp.zeros((cols, n_tok), F32)
+            for k in range(top):
+                hit = hit + (ids[k : k + 1, :] == wanted_by).astype(F32)
+            rank = contract(hit.astype(BF), before, 1, 0)
+            spot = jnp.where(hit > 0.5, rank + float(r * cap), -1.0)
+            for c in range(cols):
+                pre[c * share : (c + 1) * share, r * n_tok : (r + 1) * n_tok] = jnp.where(
+                    spots == spot[c : c + 1, :], 1.0, 0.0
+                ).astype(BF)
+
+        @pl.loop(0, cols)
+        def _(c):
+            packed[span(c, share), plane_cols] = contract(
+                pre[span(c, share), : rows * n_tok], plane[...], 1, 0
+            ).astype(BF)
+
+        for s in range(1, cols):
+            dropped(s, col, lax.rem(col + s, cols)).start()
+        own_drop().start()
+
+    def order_rows():
+        at = lax.broadcasted_iota(jnp.int32, (slots, LANES), 0).astype(F32)
+        lane_at = lax.broadcasted_iota(jnp.int32, (slots, LANES), 1).astype(F32)
+        line_of = jnp.floor((at + 0.5) * (1.0 / block))
+        rest = at - line_of * block
+        plane_of = jnp.floor((rest + 0.5) * (1.0 / cap))
+        source = plane_of * share + line_of * cap + (rest - plane_of * cap)
+        for n in range(slots // LANES):
+            pre[:, n * LANES : (n + 1) * LANES] = jnp.where(
+                lane_at + float(n * LANES) == source, 1.0, 0.0
+            ).astype(BF)
+
+    def project_plane():
+        loads[n_first].wait()
+        own_drop().wait()
+        all_dropped().wait_recv()
+        x[:, plane_cols] = contract(pre[:, :slots], drops[...], 1, 0).astype(BF)
+
+        @pl.loop(0, 2 * ff // tile)
+        def _(n):
+            proj[:, span(n, tile)] += contract(
+                x[:, plane_cols], w[plane_cols, span(n, tile)], 1, 0
+            )
 
     gathered(0)
     spread_out(0)
@@ -645,14 +749,11 @@
     gathered(1)
     pack(0)
     send(0, mates)
+    pass_on(2)
     gathered(2)
     pack(1)
-    for kind in range(2):
-        for s in range(1, chips):
-            direct(kind, s, row, peer(s)).wait_send()
-    send(1, mates)
+    pass_on(1)
     pass_on(0)
-    pass_on(1)
     gathered(3)
     for s in mates:
         queries(s, row, flip(row, s, rows)).start()
@@ -674,14 +775,18 @@
     for c in range(cols):
         here = slice(c * n_tok, (c + 1) * n_tok)
         dmt[here, :] = dm[:, here].astype(F32).T.astype(BF)
+    spread_out(3)
+    send(1, mates)
     gathered(4)
     pack(2)
-    for s in mates:
-        scored(s, row, flip(row, s, rows)).start()
-    sent(0, mates)
-    send(2, mates)
-
     all_here(1)
+    all_here(2)
+    own_plane.wait()
+    pack_plane()
+    sent(0)
+    send(2, near)
+    order_rows()
+
     lines = rows * cols
     each = lax.broadcasted_iota(jnp.int32, (lines, n_tok), 0)
     mine = me.astype(F32)
@@ -711,15 +816,9 @@
             ).astype(BF)
         spread[span(r, block), :] = contract(placed[...], group[...], 1, 0).astype(BF)
 
-    gathered(5)
-    pack(3)
     project(0)
-    sent(1, mates)
-    send(3, near)
-    project(1)
-    for s in mates:
-        origin = flip(row, s, rows)
-        scored(s, origin, origin).wait_recv()
+    pass_on(3)
+    all_here(3)
 
     @pl.loop(0, width // tile)
     def _(n):
@@ -727,7 +826,7 @@
             contract(dsc[...], docs[:, span(n, tile)], 1, 0) / SEQ_LEN
         ).astype(BF)
 
-    loads[n_first].wait()
+    loads[n_first + 1].wait()
     small = 256
 
     @pl.loop(0, ff // small)
@@ -736,19 +835,23 @@
             cot[...], down[span(n, small), :], 1, 1
         ).astype(BF)
 
-    for s in mates:
-        origin = flip(row, s, rows)
-        queries(s, origin, origin).wait_recv()
+    all_queries().wait_recv()
     own_queries().wait()
     passage_ref[...] = contract(dsc[:, span(col, n_doc)], qcols[...], 0, 0)
-    sent(2, mates)
-    send(3, far)
-    project(2)
+    sent(1)
+    send(2, far)
+    project(1)
+    project_plane()
 
     def returning(f, s, origin, to):
         part = pl.ds(*last[f])
         return remote(packed.at[span(to, block), part], ret.at[span(origin, block), part],
-                      es.at[f, s], er.at[f, origin], (to, col))
+                      es.at[f], er.at[f], (to, col))
+
+    def all_returned(f):
+        part = pl.ds(*last[f])
+        here = pl.ds(0, (rows - 1) * block)
+        return remote(packed.at[here, part], ret.at[here, part], es.at[f], er.at[f], (row, col))
 
     def held(f):
         part = pl.ds(*last[f])
@@ -760,21 +863,25 @@
     def home(f, s, origin, to):
         part = pl.ds(*last[f])
         return remote(comb.at[span(to, n_tok), part], parts.at[origin, :, part],
-                      fs.at[f, s], fr.at[f, origin], (row, to))
+                      fs.at[f], fr.at[f], (row, to))
+
+    def all_home(f):
+        part = pl.ds(*last[f])
+        here = pl.ds(0, cols - 1)
+        return remote(parts.at[here, :, part], parts.at[here, :, part], fs.at[f], fr.at[f], (row, col))
 
     f_end = n_first - 1
     loads[f_end].wait()
     kept(f_end).wait()
     end = pl.ds(*first[f_end])
-    begin_cols = pl.ds(*last[0])
+    lead = 2
+    begin_cols = pl.ds(0, last[0][1] + last[1][1])
     lane = 128
 
-    for s in range(chips):
+    for s in [k for k in (1, 2, 0, 3) if k < chips]:
         other = flip(chip, s, chips)
-        for k in (2 * s, 2 * s + 1):
-            if k:
-                origin = flip(row, k, rows)
-                outgoing(f_end, k, origin, origin).wait_recv()
+        count = 2 if s else 1
+        batch(f_end, count, ds.at[f_end], dr.at[f_end + s]).wait_recv()
         here = span(other, pair)
 
         @pl.loop(0, 2 * ff // tile)
@@ -799,18 +906,15 @@
                 pre[at, right] = (grad * act).astype(BF)
 
         packed[here, begin_cols] = contract(pre[here, :], w[begin_cols, :], 1, 1).astype(BF)
-        for k in (2 * s, 2 * s + 1):
-            if k:
-                returning(0, k, row, flip(row, k, rows)).start()
-            else:
-                held(0).start()
-
-    flushed = False
-    for f in range(1, n_last):
+        for f in range(lead):
+            for k in (2 * s, 2 * s + 1):
+                if k:
+                    returning(f, k, row, flip(row, k, rows)).start()
+                else:
+                    held(f).start()
+
+    def give_back(f):
         at, size = last[f]
-        if at + size > first[final][0] and not flushed:
-            flushed = True
-            sent(final, near + far)
         bit = math.gcd(size, small)
 
         @pl.loop(0, size // bit)
@@ -822,11 +926,12 @@
             returning(f, s, row, flip(row, s, rows)).start()
         held(f).start()
 
-    @pl.loop(0, rows)
-    def _(r):
-        hbq[span(r, line_q), :] = contract(
-            spread[span(r, block), :], hidden[span(r, block), :], 0, 0
-        ).astype(BF)
+    ahead = lead + 3
+    sent(final)
+    sent(final, late=True)
+    all_dropped().wait_send()
+    for f in range(lead, ahead):
+        give_back(f)
 
     n_gate, n_down = width // small, ff // small
 
@@ -859,9 +964,7 @@
 
     def merge(f):
         held(f).wait()
-        for s in range(1, rows):
-            origin = flip(row, s, rows)
-            returning(f, s, origin, origin).wait_recv()
+        all_returned(f).wait_recv()
         part = pl.ds(*last[f])
         comb[:, part] = contract(dmt[...], ret[:, part], 1, 0).astype(BF)
         for s in range(1, cols):
@@ -873,50 +976,57 @@
         == lax.broadcasted_iota(jnp.int32, (n_tok, per_dev), 1)
     ).astype(BF)
 
+    def leaving(f):
+        part = pl.ds(*last[f])
+        return pltpu.make_async_copy(sums_out.at[:, part], out_ref.at[:, part], leave_sem.at[f])
+
     def finish(f):
         part = pl.ds(*last[f])
         sums = contract(repeat, cot[span(me, per_dev), part], 1, 0)
         sums = sums + comb[span(col, n_tok), part].astype(F32)
+        all_home(f).wait_recv()
         for s in range(1, cols):
             origin = lax.rem(col + s, cols)
-            home(f, s, origin, origin).wait_recv()
             sums = sums + parts[origin, :, part].astype(F32)
-        out_ref[:, part] = sums.astype(BF)
+        sums_out[:, part] = sums.astype(BF)
+        leaving(f).start()
 
     tiles = n_gate + n_down
     done = 0
     for f in range(n_last):
         merge(f)
+        if f + ahead < n_last:
+            give_back(f + ahead)
         if f >= 1:
             finish(f - 1)
         if f == 0:
-            for kind in range(2):
-                for s in range(1, chips):
-                    relay(kind, s, peer(s)).wait_send()
-                direct(kind, 0, row, sibling).wait_send()
+            @pl.loop(0, rows)
+            def _(r):
+                hbq[span(r, line_q), :] = contract(
+                    spread[span(r, block), :], hidden[span(r, block), :], 0, 0
+                ).astype(BF)
+
+            for kind in range(4):
+                all_out(kind)
+                passed(kind)
             for kind in range(3 + n_first):
                 settle(kind)
-            for s in mates:
-                to = flip(row, s, rows)
-                queries(s, row, to).wait_send()
-                scored(s, row, to).wait_send()
-        until = min(tiles, -(-tiles * (f + 1) // 3))
+            all_queries().wait_send()
+        until = min(tiles, 2 * f)
         for i in range(done, until):
             grad_tile(i)
         done = until
-    finish(n_last - 1)
     for i in range(tiles - 2, tiles):
         grad_out(i).wait()
+    finish(n_last - 1)
 
     for f in range(n_last):
-        for s in mates:
-            returning(f, s, row, flip(row, s, rows)).wait_send()
-    for f in range(n_last):
-        for s in range(1, cols):
-            home(f, s, col, lax.rem(col + s, cols)).wait_send()
-
-
-def fused_plan(rows, cols, cap, top, tokens, documents, questions, down):
+        all_returned(f).wait_send()
+        all_home(f).wait_send()
+        leaving(f).wait()
+
+
+def fused_plan(rows, cols, cap, top, plane_width, tokens, documents, questions, down):
     n_tok, width = tokens.shape
     n_doc, w_doc = documents.shape
     n_qry = questions.shape[0]
@@ -930,7 +1040,7 @@
     return [
         ((2 * top, n_tok), F32),
         ((rows * cols, 2 * top, n_tok), F32),
-        ((line, width), BF),
+        ((line, width - plane_width), BF),
         ((slots, width), BF),
         ((slots, width), BF),
         ((width, 2 * ff), BF),
@@ -957,6 +1067,9 @@
         ((cols, n_tok, width), BF),
         ((n_all, ff), BF),
         ((2, stage_rows, max(width, 2 * ff)), BF),
+        ((rows * n_tok, plane_width), BF),
+        ((slots, plane_width), BF),
+        ((n_tok, width), BF),
     ]
 
 
@@ -968,14 +1081,15 @@
     n_tok, width = tokens.shape
     n_doc, w_doc = documents.shape
     hidden2 = gate_up.shape[1]
-    first = [width // 4] * 4
-    last = [width // 4] * 3 + [width // 8] * 2
+    first = [width // 4] * 3
+    plane_width = width - sum(first)
+    last = [width // 8] * 7 + [width // 16] * 2
     dma = pltpu.SemaphoreType.DMA
     vmem = pl.BlockSpec(memory_space=pltpu.VMEM)
     hbm = pl.BlockSpec(memory_space=pl.ANY)
     n_first, n_last = len(first), len(last)
     return pl.pallas_call(
-        functools.partial(fused_kernel, rows, cols, cap, first, last),
+        functools.partial(fused_kernel, rows, cols, cap, first, plane_width, last),
         out_shape=(
             jax.ShapeDtypeStruct((n_doc, w_doc), F32),
             jax.ShapeDtypeStruct((n_tok, width), BF),
@@ -983,27 +1097,28 @@
             jax.ShapeDtypeStruct(down.shape, BF),
         ),
         in_specs=[vmem] * 6 + [hbm] * 2,
-        out_specs=[vmem, vmem, hbm, hbm],
+        out_specs=[vmem, hbm, hbm, hbm],
         scratch_shapes=[pltpu.VMEM(shape, kind) for shape, kind in plan]
         + [
-            dma((4 + 2 * n_first + n_last,)),
+            dma((6 + 2 * n_first + n_last,)),
+            dma((n_first + 2,)),
+            dma((3 + n_first, 2)),
+            dma((3 + n_first, cols)),
+            dma((4,)),
+            dma((4, 2)),
+            dma((4,)),
             dma((n_first + 1,)),
-            dma((3 + n_first, 2, cols)),
-            dma((3 + n_first, cols)),
-            dma((2, rows)),
-            dma((2, rows)),
-            dma((2, rows)),
-            dma((n_first, rows)),
-            dma((n_first, rows)),
-            dma((rows,)),
-            dma((rows,)),
-            dma((rows,)),
-            dma((rows,)),
-            dma((n_last, rows)),
-            dma((n_last, rows)),
-            dma((n_last, cols)),
-            dma((n_last, cols)),
+            dma((n_first + rows // 2,)),
+            dma((1,)),
+            dma((1,)),
+            dma((1,)),
+            dma((1,)),
+            dma((n_last,)),
+            dma((n_last,)),
+            dma((n_last,)),
+            dma((n_last,)),
             dma((2,)),
+            dma((n_last,)),
         ],
         compiler_params=pltpu.CompilerParams(
             collective_id=2, has_side_effects=True, vmem_limit_bytes=VMEM_LIMIT
@@ -1039,7 +1154,7 @@
 
 
 def settled(*arrays):
-    halves = [a.size * a.dtype.itemsize // (1 << 19) for a in arrays]
+    halves = [a.size * a.dtype.itemsize // (1 << 18) for a in arrays]
     pieces = [1 << max(0, n.bit_length() - 1) for n in halves]
     dma = pltpu.SemaphoreType.DMA
     hbm = pl.BlockSpec(memory_space=pl.ANY)
@@ -1080,7 +1195,7 @@
     gate_up = expert_gate_up[0]
     down = expert_down[0]
 
-    plan = fused_plan(rows, cols, cap, top, tokens, document_vectors, question_vectors, down)
+    plan = fused_plan(rows, cols, cap, top, width // 4, tokens, document_vectors, question_vectors, down)
     if rows == 8 and plan_bytes(plan) < VMEM_LIMIT - 6_000_000:
         passage_grad, token_grad, gate_up_grad, down_grad = fused(
             rows, cols, cap, plan, tokens, document_vectors, question_vectors, positive,

time: 164 us -> 152 us (0.927)
  Pallas kernels: 163 us -> 150 us
    pallas_call x1, Pallas kernels: 155 us -> 142 us  [fused(): pl.pallas_call(functools.partial(fused_kernel, rows, cols, cap, first, pl...]
where the time goes in v3:
time: 152 us; the launch traced here: 151 us
  Pallas kernels  150 us (99%)
    pallas_call x1, Pallas kernels, fused(): pl.pallas_call(functools.partial(fused_kernel, rows, cols, cap, first, pl...  142 us
    pallas_call x1, Pallas kernels, settled(): pl.pallas_call(functools.partial(settle_kernel, pieces), out_shape=tuple(...  7.9 us

profile of v3, /device:TPU:0, one launch (start us, length us, event | category | flops | bytes accessed | tf_op | source)
XLA Modules:
  0.0 150.8 jit_solution(13741049312465740093)
XLA Ops:
  0.6 142.1 %fused.1 = (f32[128,256]{1,0:T(8,128)}, bf16[128,2048]{1,0:T(8,128)(2,1)}, bf16[2048,1536]{1,0:T(8,128)(2,1)}, bf16[768,2048]{1,0:T(8,128)(2,1)}) custom-call(bf16[128,2048]{1,0:T(8,128)(2,1)} %tok_ref.1, bf16[128,256]{1,0:T(8,128)(2,1)} %doc_ref.1, bf16[64,512]{1,0:T(8,128)(2,1)} %qry_ref.1, s32[1,64]{1,0:T(1,128)} %bitcast.11, s32[8,128]{1,0:T(8,128)} %bitcast.9, ...), custom_call_target="tpu_custom_call" | custom-call | tf_op jit(solution)/shard_map/fused/pallas_call | solution.py:1091
  142.7 7.9 %settle.1 = (f32[128,256]{1,0:T(8,128)}, bf16[128,2048]{1,0:T(8,128)(2,1)}, bf16[2048,1536]{1,0:T(8,128)(2,1)}, bf16[768,2048]{1,0:T(8,128)(2,1)}) custom-call(f32[128,256]{1,0:T(8,128)} %get-tuple-element.12.refs_0_, bf16[128,2048]{1,0:T(8,128)(2,1)} %get-tuple-element.13.refs_1_, bf16[2048,1536]{1,0:T(8,128)(2,1)} %get-tuple-element.14.refs_2_, ...), custom_call_target="tpu_custom_call" | custom-call | tf_op jit(solution)/shard_map/settle/pallas_call | solution.py:1161

commit v4 on v3

--- a/solution.py
+++ b/solution.py
@@ -12,6 +12,7 @@
 LANES = 128
 CHUNKS = 4
 VMEM_LIMIT = 67_000_000
+FUSED_LIMIT = 56_600_000
 
 sharpness_divisor = 0.02
 
@@ -404,12 +405,11 @@
 def fused_kernel(
     rows, cols, cap, first_widths, plane_width, last_widths,
     tok_ref, doc_ref, qry_ref, pos_ref, ids_ref, rw_ref, wgu_ref, down_ref,
-    passage_ref, out_ref, gug_ref, dg_ref,
-    meta, metas, tokc, packed, x, w, down, proj, dm, dmt, place, weight, placed, group,
+    passage_ref, out_ref, w, down,
+    meta, metas, tokc, packed, x, proj, dm, dmt, place, weight, placed, group,
     docs, qrow, qcols, dsc, cot, cot_down, spread, hgrad, hidden, pre, ret, comb, parts,
-    hbq, stage, plane, drops, sums_out,
-    own_sem, load_sem, zs, zr, gs, gr, rs, ds, dr, qs, qr, ps, pr, es, er, fs, fr, out_sem,
-    leave_sem,
+    hbq, plane, drops,
+    own_sem, load_sem, zs, zr, gs, gr, rs, ds, dr, qs, qr, ps, pr, es, er, fs, fr,
 ):
     row, col = lax.axis_index("row"), lax.axis_index("col")
     me = row * cols + col
@@ -701,6 +701,7 @@
                 pre[span(c, share), : rows * n_tok], plane[...], 1, 0
             ).astype(BF)
 
+        settle(2 + n_first)
         for s in range(1, cols):
             dropped(s, col, lax.rem(col + s, cols)).start()
         own_drop().start()
@@ -755,9 +756,6 @@
     pass_on(1)
     pass_on(0)
     gathered(3)
-    for s in mates:
-        queries(s, row, flip(row, s, rows)).start()
-    own_queries().start()
     all_here(0)
     scores = contract(qrow[...], docs[...], 1, 1) / sharpness_divisor
     peak = jnp.max(scores, axis=1, keepdims=True)
@@ -776,13 +774,15 @@
         here = slice(c * n_tok, (c + 1) * n_tok)
         dmt[here, :] = dm[:, here].astype(F32).T.astype(BF)
     spread_out(3)
-    send(1, mates)
+    send(1, near)
     gathered(4)
     pack(2)
+    send(1, far)
     all_here(1)
     all_here(2)
     own_plane.wait()
     pack_plane()
+    pass_on(3)
     sent(0)
     send(2, near)
     order_rows()
@@ -817,7 +817,6 @@
         spread[span(r, block), :] = contract(placed[...], group[...], 1, 0).astype(BF)
 
     project(0)
-    pass_on(3)
     all_here(3)
 
     @pl.loop(0, width // tile)
@@ -835,11 +834,11 @@
             cot[...], down[span(n, small), :], 1, 1
         ).astype(BF)
 
-    all_queries().wait_recv()
-    own_queries().wait()
-    passage_ref[...] = contract(dsc[:, span(col, n_doc)], qcols[...], 0, 0)
     sent(1)
     send(2, far)
+    for s in mates:
+        queries(s, row, flip(row, s, rows)).start()
+    own_queries().start()
     project(1)
     project_plane()
 
@@ -874,11 +873,15 @@
     loads[f_end].wait()
     kept(f_end).wait()
     end = pl.ds(*first[f_end])
-    lead = 2
-    begin_cols = pl.ds(0, last[0][1] + last[1][1])
+    groups = [[0, 1], [2, 3], [4, 5], list(range(6, n_last))]
+
+    def group_cols(g):
+        return pl.ds(last[groups[g][0]][0], sum(last[f][1] for f in groups[g]))
+
+    begin_cols = group_cols(0)
     lane = 128
 
-    for s in [k for k in (1, 2, 0, 3) if k < chips]:
+    for s in [k for k in (1, 2, 3, 0) if k < chips]:
         other = flip(chip, s, chips)
         count = 2 if s else 1
         batch(f_end, count, ds.at[f_end], dr.at[f_end + s]).wait_recv()
@@ -906,61 +909,40 @@
                 pre[at, right] = (grad * act).astype(BF)
 
         packed[here, begin_cols] = contract(pre[here, :], w[begin_cols, :], 1, 1).astype(BF)
-        for f in range(lead):
+        for f in groups[0]:
             for k in (2 * s, 2 * s + 1):
                 if k:
                     returning(f, k, row, flip(row, k, rows)).start()
                 else:
                     held(f).start()
 
-    def give_back(f):
-        at, size = last[f]
-        bit = math.gcd(size, small)
-
-        @pl.loop(0, size // bit)
-        def _(n):
-            part = pl.ds(pl.multiple_of(at + n * bit, bit), bit)
-            packed[:, part] = contract(pre[...], w[part, :], 1, 1).astype(BF)
-
-        for s in mates:
-            returning(f, s, row, flip(row, s, rows)).start()
-        held(f).start()
-
-    ahead = lead + 3
-    sent(final)
-    sent(final, late=True)
-    all_dropped().wait_send()
-    for f in range(lead, ahead):
-        give_back(f)
+    def give_back(g):
+        part = group_cols(g)
+        if g == 2:
+            sent(final)
+            sent(final, late=True)
+        if g == 3:
+            all_dropped().wait_send()
+
+        @pl.loop(0, 2)
+        def _(m):
+            half = span(m, slots // 2)
+            packed[half, part] = contract(pre[half, :], w[part, :], 1, 1).astype(BF)
+
+        for f in groups[g]:
+            for s in mates:
+                returning(f, s, row, flip(row, s, rows)).start()
+            held(f).start()
 
     n_gate, n_down = width // small, ff // small
 
-    def gate_out(i):
-        return pltpu.make_async_copy(
-            stage.at[i % 2, :, pl.ds(0, 2 * ff)], gug_ref.at[pl.ds(i * small, small)],
-            out_sem.at[i % 2],
-        )
-
-    def down_out(i):
-        j = n_gate + i
-        return pltpu.make_async_copy(
-            stage.at[j % 2], dg_ref.at[pl.ds(i * small, small)], out_sem.at[j % 2]
-        )
-
-    def grad_out(i):
-        return gate_out(i) if i < n_gate else down_out(i - n_gate)
-
     def grad_tile(i):
-        if i >= 2:
-            grad_out(i - 2).wait()
         if i < n_gate:
-            stage[i % 2, :, : 2 * ff] = contract(
-                x[:, i * small : (i + 1) * small], pre[...], 0, 0
-            ).astype(BF)
+            here = slice(i * small, (i + 1) * small)
+            w[here, :] = contract(x[:, here], pre[...], 0, 0).astype(BF)
         else:
-            j = i - n_gate
-            stage[i % 2] = contract(hbq[:, j * small : (j + 1) * small], cot[...], 0, 0).astype(BF)
-        grad_out(i).start()
+            here = slice((i - n_gate) * small, (i - n_gate + 1) * small)
+            down[here, :] = contract(hbq[:, here], cot[...], 0, 0).astype(BF)
 
     def merge(f):
         held(f).wait()
@@ -975,10 +957,6 @@
         lax.broadcasted_iota(jnp.int32, (n_tok, per_dev), 0) // SEQ_LEN
         == lax.broadcasted_iota(jnp.int32, (n_tok, per_dev), 1)
     ).astype(BF)
-
-    def leaving(f):
-        part = pl.ds(*last[f])
-        return pltpu.make_async_copy(sums_out.at[:, part], out_ref.at[:, part], leave_sem.at[f])
 
     def finish(f):
         part = pl.ds(*last[f])
@@ -988,42 +966,57 @@
         for s in range(1, cols):
             origin = lax.rem(col + s, cols)
             sums = sums + parts[origin, :, part].astype(F32)
-        sums_out[:, part] = sums.astype(BF)
-        leaving(f).start()
-
-    tiles = n_gate + n_down
-    done = 0
-    for f in range(n_last):
+        out_ref[:, part] = sums.astype(BF)
+
+    def by_query():
+        @pl.loop(0, rows)
+        def _(r):
+            hbq[span(r, line_q), :] = contract(
+                spread[span(r, block), :], hidden[span(r, block), :], 0, 0
+            ).astype(BF)
+
+    def settle_sends():
+        for kind in range(4):
+            all_out(kind)
+            passed(kind)
+        for kind in range(2 + n_first):
+            settle(kind)
+        all_queries().wait_send()
+
+    todo = list(range(n_gate, n_gate + n_down)) + list(range(n_gate))
+
+    def grads(count):
+        for i in todo[:count]:
+            grad_tile(i)
+        del todo[:count]
+
+    give_back(1)
+    merge(0)
+    give_back(2)
+    merge(1)
+    by_query()
+    finish(0)
+    all_queries().wait_recv()
+    own_queries().wait()
+    passage_ref[...] = contract(dsc[:, span(col, n_doc)], qcols[...], 0, 0)
+    settle_sends()
+    grads(2)
+    merge(2)
+    finish(1)
+    give_back(3)
+    for f in range(3, n_last - 2):
+        grads(2)
         merge(f)
-        if f + ahead < n_last:
-            give_back(f + ahead)
-        if f >= 1:
-            finish(f - 1)
-        if f == 0:
-            @pl.loop(0, rows)
-            def _(r):
-                hbq[span(r, line_q), :] = contract(
-                    spread[span(r, block), :], hidden[span(r, block), :], 0, 0
-                ).astype(BF)
-
-            for kind in range(4):
-                all_out(kind)
-                passed(kind)
-            for kind in range(3 + n_first):
-                settle(kind)
-            all_queries().wait_send()
-        until = min(tiles, 2 * f)
-        for i in range(done, until):
-            grad_tile(i)
-        done = until
-    for i in range(tiles - 2, tiles):
-        grad_out(i).wait()
-    finish(n_last - 1)
+        finish(f - 1)
+    grads(len(todo))
+    for f in range(n_last - 2, n_last):
+        merge(f)
+    for f in range(n_last - 3, n_last):
+        finish(f)
 
     for f in range(n_last):
         all_returned(f).wait_send()
         all_home(f).wait_send()
-        leaving(f).wait()
 
 
 def fused_plan(rows, cols, cap, top, plane_width, tokens, documents, questions, down):
@@ -1036,15 +1029,12 @@
     line = cols * n_tok
     line_q = line // SEQ_LEN
     n_all = rows * n_qry
-    stage_rows = 256
     return [
         ((2 * top, n_tok), F32),
         ((rows * cols, 2 * top, n_tok), F32),
         ((line, width - plane_width), BF),
         ((slots, width), BF),
         ((slots, width), BF),
-        ((width, 2 * ff), BF),
-        ((ff, width), BF),
         ((slots, 2 * ff), F32),
         ((slots, line), BF),
         ((line, slots), BF),
@@ -1066,10 +1056,8 @@
         ((line, width), BF),
         ((cols, n_tok, width), BF),
         ((n_all, ff), BF),
-        ((2, stage_rows, max(width, 2 * ff)), BF),
         ((rows * n_tok, plane_width), BF),
         ((slots, plane_width), BF),
-        ((n_tok, width), BF),
     ]
 
 
@@ -1081,7 +1069,7 @@
     n_tok, width = tokens.shape
     n_doc, w_doc = documents.shape
     hidden2 = gate_up.shape[1]
-    first = [width // 4] * 3
+    first = [width * k // 16 for k in (4, 5, 4)]
     plane_width = width - sum(first)
     last = [width // 8] * 7 + [width // 16] * 2
     dma = pltpu.SemaphoreType.DMA
@@ -1091,13 +1079,13 @@
     return pl.pallas_call(
         functools.partial(fused_kernel, rows, cols, cap, first, plane_width, last),
         out_shape=(
-            jax.ShapeDtypeStruct((n_doc, w_doc), F32),
-            jax.ShapeDtypeStruct((n_tok, width), BF),
-            jax.ShapeDtypeStruct((width, hidden2), BF),
-            jax.ShapeDtypeStruct(down.shape, BF),
+            pltpu.VMEM((n_doc, w_doc), F32),
+            pltpu.VMEM((n_tok, width), BF),
+            pltpu.VMEM((width, hidden2), BF),
+            pltpu.VMEM(down.shape, BF),
         ),
         in_specs=[vmem] * 6 + [hbm] * 2,
-        out_specs=[vmem, hbm, hbm, hbm],
+        out_specs=[vmem] * 4,
         scratch_shapes=[pltpu.VMEM(shape, kind) for shape, kind in plan]
         + [
             dma((6 + 2 * n_first + n_last,)),
@@ -1117,11 +1105,9 @@
             dma((n_last,)),
             dma((n_last,)),
             dma((n_last,)),
-            dma((2,)),
-            dma((n_last,)),
         ],
         compiler_params=pltpu.CompilerParams(
-            collective_id=2, has_side_effects=True, vmem_limit_bytes=VMEM_LIMIT
+            collective_id=2, has_side_effects=True, vmem_limit_bytes=FUSED_LIMIT
         ),
         name="fused",
     )(tokens, documents, questions, positive.reshape(1, -1), ids.T, weights.T, gate_up, down)
@@ -1129,45 +1115,35 @@
 
 def settle_kernel(pieces, *refs):
     count = len(pieces)
-    sources, targets = refs[:count], refs[count : 2 * count]
-    buffers, in_sem, out_sem = refs[2 * count : 3 * count], refs[-2], refs[-1]
-    todo = []
+    sources, targets, sem = refs[:count], refs[count:-1], refs[-1]
+    copies = []
     for i, parts in enumerate(pieces):
         size = sources[i].shape[0] // parts
         for p in range(parts):
-            todo.append((i, pl.ds(p * size, size)))
-    ins = [
-        pltpu.make_async_copy(sources[i].at[at], buffers[i].at[at], in_sem.at[n])
-        for n, (i, at) in enumerate(todo)
-    ]
-    outs = [
-        pltpu.make_async_copy(buffers[i].at[at], targets[i].at[at], out_sem.at[n])
-        for n, (i, at) in enumerate(todo)
-    ]
-    for copy in ins:
+            at = pl.ds(p * size, size)
+            copies.append(
+                pltpu.make_async_copy(sources[i].at[at], targets[i].at[at], sem.at[len(copies)])
+            )
+    for copy in copies:
         copy.start()
-    for arrived, leave in zip(ins, outs):
-        arrived.wait()
-        leave.start()
-    for copy in outs:
+    for copy in copies:
         copy.wait()
 
 
 def settled(*arrays):
-    halves = [a.size * a.dtype.itemsize // (1 << 18) for a in arrays]
-    pieces = [1 << max(0, n.bit_length() - 1) for n in halves]
-    dma = pltpu.SemaphoreType.DMA
+    sizes = [a.size * a.dtype.itemsize // (1 << 20) for a in arrays]
+    pieces = [1 << max(0, n.bit_length() - 1) for n in sizes]
+    vmem = pl.BlockSpec(memory_space=pltpu.VMEM)
     hbm = pl.BlockSpec(memory_space=pl.ANY)
     return pl.pallas_call(
         functools.partial(settle_kernel, pieces),
-        out_shape=tuple(jax.ShapeDtypeStruct(a.shape, a.dtype) for a in arrays),
-        in_specs=[hbm] * len(arrays),
+        out_shape=tuple(pltpu.HBM(a.shape, a.dtype) for a in arrays),
+        in_specs=[vmem] * len(arrays),
         out_specs=[hbm] * len(arrays),
-        scratch_shapes=[pltpu.VMEM(a.shape, a.dtype) for a in arrays]
-        + [dma((sum(pieces),)), dma((sum(pieces),))],
-        compiler_params=pltpu.CompilerParams(vmem_limit_bytes=VMEM_LIMIT),
+        scratch_shapes=[pltpu.SemaphoreType.DMA((sum(pieces),))],
+        compiler_params=pltpu.CompilerParams(vmem_limit_bytes=1 << 20),
         name="settle",
-    )(*arrays)
+    )(*[pltpu.with_memory_space_constraint(a, pltpu.VMEM) for a in arrays])
 
 
 def shards(
@@ -1195,8 +1171,8 @@
     gate_up = expert_gate_up[0]
     down = expert_down[0]
 
-    plan = fused_plan(rows, cols, cap, top, width // 4, tokens, document_vectors, question_vectors, down)
-    if rows == 8 and plan_bytes(plan) < VMEM_LIMIT - 6_000_000:
+    plan = fused_plan(rows, cols, cap, top, width * 3 // 16, tokens, document_vectors, question_vectors, down)
+    if rows == 8 and plan_bytes(plan) < FUSED_LIMIT - 4_000_000:
         passage_grad, token_grad, gate_up_grad, down_grad = fused(
             rows, cols, cap, plan, tokens, document_vectors, question_vectors, positive,
             expert_ids, route_weights, gate_up, down,

time: 152 us -> 141 us (0.928)
  Pallas kernels: 150 us -> 141 us
    pallas_call x1, Pallas kernels: 142 us -> 137 us  [fused(): pl.pallas_call(functools.partial(fused_kernel, rows, cols, cap, first, pl...]
    pallas_call x1, Pallas kernels: 7.9 us -> 3.93 us  [settled(): pl.pallas_call(functools.partial(settle_kernel, pieces), out_shape=tuple(...]
where the time goes in v4:
time: 141 us
  Pallas kernels  141 us (100%)
    pallas_call x1, Pallas kernels, fused(): pl.pallas_call(functools.partial(fused_kernel, rows, cols, cap, first, pl...  137 us
    pallas_call x1, Pallas kernels, settled(): pl.pallas_call(functools.partial(settle_kernel, pieces), out_shape=tuple(...  3.93 us

profile of v4, /device:TPU:0, one launch (start us, length us, event | category | flops | bytes accessed | tf_op | source)
XLA Modules:
  0.0 141.3 jit_solution(12328885100916526595)
XLA Ops:
  0.6 136.6 %fused.1 = (f32[128,256]{1,0:T(8,128)S(1)}, bf16[128,2048]{1,0:T(8,128)(2,1)S(1)}, bf16[2048,1536]{1,0:T(8,128)(2,1)S(1)}, bf16[768,2048]{1,0:T(8,128)(2,1)S(1)}) custom-call(bf16[128,2048]{1,0:T(8,128)(2,1)} %tok_ref.1, bf16[128,256]{1,0:T(8,128)(2,1)} %doc_ref.1, bf16[64,512]{1,0:T(8,128)(2,1)} %qry_ref.1, s32[1,64]{1,0:T(1,128)} %bitcast.11, ...), custom_call_target="tpu_custom_call" | custom-call | tf_op jit(solution)/shard_map/fused/pallas_call | solution.py:1079
  137.2 3.9 %settle.1 = (f32[128,256]{1,0:T(8,128)}, bf16[128,2048]{1,0:T(8,128)(2,1)}, bf16[2048,1536]{1,0:T(8,128)(2,1)}, bf16[768,2048]{1,0:T(8,128)(2,1)}) custom-call(f32[128,256]{1,0:T(8,128)S(1)} %get-tuple-element.12.refs_0_, bf16[128,2048]{1,0:T(8,128)(2,1)S(1)} %get-tuple-element.13.refs_1_, bf16[2048,1536]{1,0:T(8,128)(2,1)S(1)} %get-tuple-element.14.refs_2_, ...), custom_call_target="tpu_custom_call" | custom-call | tf_op jit(solution)/shard_map/settle/pallas_call | solution.py:1138

commit v5 on v4

--- a/solution.py
+++ b/solution.py
@@ -36,7 +36,7 @@
     )
 
 
-def greet(rows, cols):
+def greet_signal(rows, cols):
     row, col = lax.axis_index("row"), lax.axis_index("col")
     barrier = pltpu.get_barrier_semaphore()
     for s in range(1, rows):
@@ -47,7 +47,15 @@
         pl.semaphore_signal(
             barrier, inc=1, device_id=(row, lax.rem(col + s, cols)), device_id_type=MESH
         )
-    pl.semaphore_wait(barrier, rows + cols - 2)
+
+
+def greet_wait(rows, cols):
+    pl.semaphore_wait(pltpu.get_barrier_semaphore(), rows + cols - 2)
+
+
+def greet(rows, cols):
+    greet_signal(rows, cols)
+    greet_wait(rows, cols)
 
 
 def dispatch_kernel(
@@ -404,11 +412,11 @@
 
 def fused_kernel(
     rows, cols, cap, first_widths, plane_width, last_widths,
-    tok_ref, doc_ref, qry_ref, pos_ref, ids_ref, rw_ref, wgu_ref, down_ref,
+    tok_ref, doc_ref, qry_ref, pos_in, ids_in, rw_in, wgu_ref, down_ref,
     passage_ref, out_ref, w, down,
     meta, metas, tokc, packed, x, proj, dm, dmt, place, weight, placed, group,
     docs, qrow, qcols, dsc, cot, cot_down, spread, hgrad, hidden, pre, ret, comb, parts,
-    hbq, plane, drops,
+    hbq, plane, drops, pos_ref, ids_ref, rw_ref,
     own_sem, load_sem, zs, zr, gs, gr, rs, ds, dr, qs, qr, ps, pr, es, er, fs, fr,
 ):
     row, col = lax.axis_index("row"), lax.axis_index("col")
@@ -503,11 +511,19 @@
     ]
     loads.append(pltpu.make_async_copy(down_ref, down, load_sem.at[n_first + 1]))
 
-    meta[:top] = ids_ref[...].astype(F32)
-    meta[top:] = rw_ref[...]
+    greet_signal(rows, cols)
+    fetches = [
+        pltpu.make_async_copy(src, dst, load_sem.at[n_first + 2 + n])
+        for n, (src, dst) in enumerate(((ids_in, ids_ref), (rw_in, rw_ref), (pos_in, pos_ref)))
+    ]
+    for copy in fetches:
+        copy.start()
+    for copy in fetches:
+        copy.wait()
+    meta[...] = jnp.concatenate([ids_ref[...].astype(F32), rw_ref[...]], axis=0).astype(BF)
     for kind in range(3 + n_first):
         own(kind).start()
-    greet(rows, cols)
+    greet_wait(rows, cols)
     queue = [(0, 1), (3,), (4,), (2,)] + [(kind,) for kind in range(5, 3 + n_first)]
     advance(queue[0], 0)
     advance(queue[1], 0)
@@ -684,7 +700,7 @@
         ).astype(F32)
         spots = lax.broadcasted_iota(jnp.int32, (share, n_tok), 0).astype(F32)
         for r in range(rows):
-            ids = metas[r * cols + col, :top]
+            ids = metas[r * cols + col].astype(F32)
             hit = jnp.zeros((cols, n_tok), F32)
             for k in range(top):
                 hit = hit + (ids[k : k + 1, :] == wanted_by).astype(F32)
@@ -701,7 +717,6 @@
                 pre[span(c, share), : rows * n_tok], plane[...], 1, 0
             ).astype(BF)
 
-        settle(2 + n_first)
         for s in range(1, cols):
             dropped(s, col, lax.rem(col + s, cols)).start()
         own_drop().start()
@@ -737,7 +752,7 @@
         lax.broadcasted_iota(jnp.int32, (rows, n_tok), 0) * cols + col
     ).astype(F32)
     for c in range(cols):
-        ids = metas[row * cols + c, :top]
+        ids = metas[row * cols + c].astype(F32)
         hit = jnp.zeros((rows, n_tok), F32)
         for k in range(top):
             hit = hit + (ids[k : k + 1, :] == target).astype(F32)
@@ -775,9 +790,9 @@
         dmt[here, :] = dm[:, here].astype(F32).T.astype(BF)
     spread_out(3)
     send(1, near)
+    send(1, far)
     gathered(4)
     pack(2)
-    send(1, far)
     all_here(1)
     all_here(2)
     own_plane.wait()
@@ -793,9 +808,10 @@
     chosen = jnp.zeros((lines, n_tok), F32)
     amount = jnp.zeros((lines, n_tok), F32)
     for b in range(lines):
-        hit = (metas[b, :top] == mine).astype(F32)
+        entry = metas[b].astype(F32)
+        hit = (entry[:top] == mine).astype(F32)
         found = jnp.sum(hit, axis=0, keepdims=True)
-        value = jnp.sum(hit * metas[b, top:], axis=0, keepdims=True)
+        value = jnp.sum(hit * entry[top:], axis=0, keepdims=True)
         chosen = jnp.where(each == b, found, chosen)
         amount = jnp.where(each == b, value, amount)
     rank = contract(chosen.astype(BF), before, 1, 0)
@@ -979,7 +995,7 @@
         for kind in range(4):
             all_out(kind)
             passed(kind)
-        for kind in range(2 + n_first):
+        for kind in range(3 + n_first):
             settle(kind)
         all_queries().wait_send()
 
@@ -990,28 +1006,27 @@
             grad_tile(i)
         del todo[:count]
 
+    merge(0)
     give_back(1)
-    merge(0)
+    merge(1)
     give_back(2)
-    merge(1)
     by_query()
-    finish(0)
     all_queries().wait_recv()
     own_queries().wait()
     passage_ref[...] = contract(dsc[:, span(col, n_doc)], qcols[...], 0, 0)
     settle_sends()
     grads(2)
     merge(2)
-    finish(1)
+    finish(0)
     give_back(3)
     for f in range(3, n_last - 2):
         grads(2)
         merge(f)
-        finish(f - 1)
+        finish(f - 2)
     grads(len(todo))
     for f in range(n_last - 2, n_last):
         merge(f)
-    for f in range(n_last - 3, n_last):
+    for f in range(n_last - 4, n_last):
         finish(f)
 
     for f in range(n_last):
@@ -1030,8 +1045,8 @@
     line_q = line // SEQ_LEN
     n_all = rows * n_qry
     return [
-        ((2 * top, n_tok), F32),
-        ((rows * cols, 2 * top, n_tok), F32),
+        ((2 * top, n_tok), BF),
+        ((rows * cols, 2 * top, n_tok), BF),
         ((line, width - plane_width), BF),
         ((slots, width), BF),
         ((slots, width), BF),
@@ -1058,6 +1073,9 @@
         ((n_all, ff), BF),
         ((rows * n_tok, plane_width), BF),
         ((slots, plane_width), BF),
+        ((1, n_qry), jnp.int32),
+        ((top, n_tok), jnp.int32),
+        ((top, n_tok), F32),
     ]
 
 
@@ -1069,7 +1087,7 @@
     n_tok, width = tokens.shape
     n_doc, w_doc = documents.shape
     hidden2 = gate_up.shape[1]
-    first = [width * k // 16 for k in (4, 5, 4)]
+    first = [width * k // 16 for k in (4, 4, 4)]
     plane_width = width - sum(first)
     last = [width // 8] * 7 + [width // 16] * 2
     dma = pltpu.SemaphoreType.DMA
@@ -1084,12 +1102,12 @@
             pltpu.VMEM((width, hidden2), BF),
             pltpu.VMEM(down.shape, BF),
         ),
-        in_specs=[vmem] * 6 + [hbm] * 2,
+        in_specs=[hbm] * 8,
         out_specs=[vmem] * 4,
         scratch_shapes=[pltpu.VMEM(shape, kind) for shape, kind in plan]
         + [
             dma((6 + 2 * n_first + n_last,)),
-            dma((n_first + 2,)),
+            dma((n_first + 5,)),
             dma((3 + n_first, 2)),
             dma((3 + n_first, cols)),
             dma((4,)),
@@ -1131,7 +1149,7 @@
 
 
 def settled(*arrays):
-    sizes = [a.size * a.dtype.itemsize // (1 << 20) for a in arrays]
+    sizes = [a.size * a.dtype.itemsize // (1 << 18) for a in arrays]
     pieces = [1 << max(0, n.bit_length() - 1) for n in sizes]
     vmem = pl.BlockSpec(memory_space=pltpu.VMEM)
     hbm = pl.BlockSpec(memory_space=pl.ANY)
@@ -1171,8 +1189,8 @@
     gate_up = expert_gate_up[0]
     down = expert_down[0]
 
-    plan = fused_plan(rows, cols, cap, top, width * 3 // 16, tokens, document_vectors, question_vectors, down)
-    if rows == 8 and plan_bytes(plan) < FUSED_LIMIT - 4_000_000:
+    plan = fused_plan(rows, cols, cap, top, width * 4 // 16, tokens, document_vectors, question_vectors, down)
+    if rows == 8 and experts_all <= 256 and plan_bytes(plan) < FUSED_LIMIT - 4_000_000:
         passage_grad, token_grad, gate_up_grad, down_grad = fused(
             rows, cols, cap, plan, tokens, document_vectors, question_vectors, positive,
             expert_ids, route_weights, gate_up, down,

time: 141 us -> 140 us (level)
  Pallas kernels: 141 us -> 139 us
    pallas_call x1, Pallas kernels: 137 us -> 135 us  [fused(): pl.pallas_call(functools.partial(fused_kernel, rows, cols, cap, first, pl...]
where the time goes in v5:
time: 140 us
  Pallas kernels  139 us (99%)
    pallas_call x1, Pallas kernels, fused(): pl.pallas_call(functools.partial(fused_kernel, rows, cols, cap, first, pl...  135 us
    pallas_call x1, Pallas kernels, settled(): pl.pallas_call(functools.partial(settle_kernel, pieces), out_shape=tuple(...  4.02 us

profile of v5, /device:TPU:0, one launch (start us, length us, event | category | flops | bytes accessed | tf_op | source)
XLA Modules:
  0.0 140.0 jit_solution(8124991287004248679)
XLA Ops:
  0.6 135.2 %fused.1 = (f32[128,256]{1,0:T(8,128)S(1)}, bf16[128,2048]{1,0:T(8,128)(2,1)S(1)}, bf16[2048,1536]{1,0:T(8,128)(2,1)S(1)}, bf16[768,2048]{1,0:T(8,128)(2,1)S(1)}) custom-call(bf16[128,2048]{1,0:T(8,128)(2,1)} %tok_ref.1, bf16[128,256]{1,0:T(8,128)(2,1)} %doc_ref.1, bf16[64,512]{1,0:T(8,128)(2,1)} %qry_ref.1, s32[1,64]{1,0:T(1,128)} %bitcast.11, ...), custom_call_target="tpu_custom_call" | custom-call | tf_op jit(solution)/shard_map/fused/pallas_call | solution.py:1097
  135.8 4.0 %settle.1 = (f32[128,256]{1,0:T(8,128)}, bf16[128,2048]{1,0:T(8,128)(2,1)}, bf16[2048,1536]{1,0:T(8,128)(2,1)}, bf16[768,2048]{1,0:T(8,128)(2,1)}) custom-call(f32[128,256]{1,0:T(8,128)S(1)} %get-tuple-element.12.refs_0_, bf16[128,2048]{1,0:T(8,128)(2,1)S(1)} %get-tuple-element.13.refs_1_, bf16[2048,1536]{1,0:T(8,128)(2,1)S(1)} %get-tuple-element.14.refs_2_, ...), custom_call_target="tpu_custom_call" | custom-call | tf_op jit(solution)/shard_map/settle/pallas_call | solution.py:1156
